TPU v7x, 32 devices: a whole 2x2x4 slice. The times are simulated.
32 devices in a mesh: dp: 16 (over z, y, x), mp: 2 (over core).
Axes of the slice: x: 2, y: 2, z: 4, core: 2. Of those that a mesh axis runs over, the one named last changes fastest.
Arguments:
- hot_rows: int32 [16, 16, 32], P('dp'), may hold values from 0 to 4095
- hot_count: int32 [16, 16], P('dp'), may hold values from 1 to 32, as said below
- hot_cot: bfloat16 [16, 16, 32, 128], P('dp'), may hold values from -6 to 6
- table: float32 [65536, 128], P('dp'), may hold values from -3 to 3
- cold_ids: int32 [16384], P('dp'), may hold values from 0 to 1048575
- hash_mult: int32 [1024], replicated, may hold values from 1 to 1023
- hash_add: int32 [1024], replicated, may hold values from 0 to 1000002
- layer_one: bfloat16 [1024, 1024], P(None, 'mp'), may hold values from -0.1875 to 0.1875
- layer_two: bfloat16 [1024, 1024], P('mp'), may hold values from -0.1875 to 0.1875
- layer_three: bfloat16 [1024, 1024], P(None, 'mp'), may hold values from -0.1875 to 0.1875
- layer_four: bfloat16 [1024, 128], P('mp'), may hold values from -0.1875 to 0.1875
- cold_cot: bfloat16 [16384, 128], P('dp'), may hold values from -6 to 6
Outputs:
- hot_emb: bfloat16 [16, 16, 32, 128], P('dp')
- new_table: float32 [65536, 128], P('dp')
- cold_emb: bfloat16 [16384, 128], P('dp')
- grad_one: float32 [1024, 1024], P(None, 'mp')
- grad_two: float32 [1024, 1024], P('mp')
- grad_three: float32 [1024, 1024], P(None, 'mp')
- grad_four: float32 [1024, 128], P('mp')
Inputs may be any that keep to these rules, and one draw needn't show every extreme that they name: `hot_rows`: entries index the owner's block of 4096 rows; entries in unused slots are arbitrary. `hot_count`: every batch shard fills all 32 slots of some owner, and some owner receives 32 from every batch shard.
All inputs are finite; a program needn't handle non-finite values.
Results may differ from a plain program's by a relative error of at most 0.0074.
Values may be sent and summed in bfloat16 or wider, within the bound.
No kernel may reach another device: no remote copies, remote signals or barrier semaphores. Data moves between devices by JAX's collectives and lax.ppermute only.
A program may use at most 128 MiB of HBM per device.

v0:
```python
import functools

import jax
import jax.numpy as jnp
from jax import lax
from jax.experimental import pallas as pl
from jax.experimental.pallas import tpu as pltpu
from jax.sharding import PartitionSpec as P


learn_rate = 0.5
modulus = 1000003
BF = jnp.bfloat16
F32 = jnp.float32


def hops_of(mesh):
    count = mesh.shape["dp"]
    coords = [getattr(d, "coords", None) for d in mesh.devices[:, 0]]
    sizes = None
    if all(c is not None for c in coords):
        sizes = [len({c[axis] for c in coords}) for axis in range(3)]
        if sizes[0] * sizes[1] * sizes[2] != count:
            sizes = None
    if sizes is None:
        sizes = [2] * (count.bit_length() - 1)
    hops, base = [], 0
    for size in sizes:
        bits = size.bit_length() - 1
        assert size == 1 << bits
        if bits == 2:
            hops.append([(1 << base, 3 << base), (3 << base, 2 << base)])
        elif bits:
            hops.append([(1 << (base + k), 1 << (base + k)) for k in range(bits)])
        base += bits
    assert 1 << base == count
    flat = []
    while any(hops):
        for group in hops:
            if group:
                flat.append(group.pop(0))
    return flat


TILE = 512


def dot(a, b):
    return jnp.dot(a, b, preferred_element_type=F32)


def dot_t(a, b):
    return lax.dot_general(a, b, (((0,), (0,)), ((), ())), preferred_element_type=F32)


def dot_bt(a, b):
    return lax.dot_general(a, b, (((1,), (1,)), ((), ())), preferred_element_type=F32)


def gates(value):
    sig = jax.nn.sigmoid(value)
    return (value * sig).astype(BF), sig * (1.0 + value * (1.0 - sig))


def tiles(size, body):
    step = min(size, TILE)

    def run(j, carry):
        body(pl.ds(pl.multiple_of(j * step, step), step))
        return carry

    lax.fori_loop(0, size // step, run, 0)


class Refs:
    def __init__(self, inputs, outputs, held, kept, load_sems, store_sems):
        self.held, self.kept = held, kept
        self.loads = [pltpu.make_async_copy(s, d, load_sems.at[i]) for i, (s, d) in enumerate(zip(inputs, held))]
        self.stores = [pltpu.make_async_copy(s, d, store_sems.at[i]) for i, (s, d) in enumerate(zip(kept, outputs))]
        self.waited, self.put = set(), set()
        for load in self.loads:
            load.start()

    def need(self, *which):
        for i in which:
            if i not in self.waited:
                self.loads[i].wait()
                self.waited.add(i)
        return tuple(self.held[i] for i in which)

    def store(self, *which):
        for i in which:
            self.stores[i].start()
            self.put.add(i)

    def finish(self):
        self.need(*range(len(self.loads)))
        self.store(*(i for i in range(len(self.stores)) if i not in self.put))
        for copy in self.stores:
            copy.wait()


def call(kernel, outs, args, scratch=(), flops=0, scalars=(), shared=()):
    shapes = [jax.ShapeDtypeStruct(shape, kind) for shape, kind in outs]
    moved = sum(x.size * x.dtype.itemsize for x in list(args) + shapes)
    far = pl.BlockSpec(memory_space=pltpu.MemorySpace.HBM)
    near = pl.BlockSpec(memory_space=pltpu.SMEM)
    p, n, m = len(scalars), len(args), len(shapes)
    shared = dict(shared)
    alone = [i for i in range(n) if i not in shared]
    scalars = [jnp.asarray(x, jnp.int32).reshape(-1) for x in scalars]

    def body(*refs):
        numbers, refs = refs[:p], refs[p:]
        inputs, outputs, refs = refs[:n], refs[n : n + m], refs[n + m :]
        own, kept, rest = refs[: len(alone)], refs[len(alone) : len(alone) + m], refs[len(alone) + m :]
        own = dict(zip(alone, own))
        held = [own[i] if i in own else kept[shared[i]] for i in range(n)]
        r = Refs(inputs, outputs, held, kept, rest[-2], rest[-1])
        kernel(r, *numbers, *rest[:-2])
        r.finish()

    return pl.pallas_call(
        body,
        out_shape=shapes,
        in_specs=[near] * p + [far] * n,
        out_specs=[far] * m,
        scratch_shapes=[
            *(pltpu.VMEM(args[i].shape, args[i].dtype) for i in alone),
            *(pltpu.VMEM(x.shape, x.dtype) for x in shapes),
            *(pltpu.VMEM(shape, kind) for shape, kind in scratch),
            pltpu.SemaphoreType.DMA((n,)),
            pltpu.SemaphoreType.DMA((m,)),
        ],
        cost_estimate=pl.CostEstimate(flops=flops, bytes_accessed=moved, transcendentals=0),
    )(*scalars, *args)


def first_kernel(r, core):
    ids, mult, add = r.need(0, 1, 2)
    feats, act, slope = r.kept
    rows = feats.shape[0]
    step = min(rows, 64)

    def hash_rows(j, carry):
        at = pl.ds(pl.multiple_of(j * step, step), step)
        own = pl.ds(pl.multiple_of(core[0] * rows + j * step, step), step)
        hashed = ids[own, :] * mult[...] + add[...]
        quotient = (hashed.astype(F32) * (1.0 / modulus)).astype(jnp.int32)
        left = hashed - quotient * modulus
        left = jnp.where(left < 0, left + modulus, left)
        left = jnp.where(left >= modulus, left - modulus, left)
        feats[at, :] = (left.astype(F32) * (2.0 / 1000002.0) - 1.0).astype(BF)
        return carry

    lax.fori_loop(0, rows // step, hash_rows, 0)
    r.store(0)
    (one,) = r.need(3)

    def layer(at):
        act[:, at], slope[:, at] = gates(dot(feats[...], one[:, at]))

    tiles(one.shape[1], layer)


def second_kernel(r, core, slope_three_m, slope_three_o):
    act_o, slope_one_o, act_two, slope_two, emb, back_m, back_o, act_three_m, act_three_o = r.kept
    feats, one_o = r.need(0, 1)

    def layer_one(at):
        act_o[:, at], slope_one_o[:, at] = gates(dot(feats[...], one_o[:, at]))

    tiles(one_o.shape[1], layer_one)
    r.store(0, 1)
    act_m, two_m, two_o = r.need(2, 3, 4)

    def layer_two(at):
        act_two[:, at], slope_two[:, at] = gates(
            dot(act_m[...], two_m[:, at]) + dot(act_o[...], two_o[:, at])
        )

    tiles(two_m.shape[1], layer_two)
    r.store(2, 3)
    three_m, three_o, four_m, four_o, cots = r.need(5, 6, 7, 8, 9)
    rows = act_two.shape[0]
    cot = cots.at[pl.ds(pl.multiple_of(core[0] * rows, rows), rows), :]
    for three, four, act, slope, back, places in (
        (three_o, four_o, act_three_o, slope_three_o, back_o, (8, 6)),
        (three_m, four_m, act_three_m, slope_three_m, back_m, (7, 5)),
    ):

        def layer_three(at):
            act[:, at], slope[:, at] = gates(dot(act_two[...], three[:, at]))
            back[:, at] = (dot_bt(cot[...], four[at, :]) * slope[:, at]).astype(BF)

        tiles(three.shape[1], layer_three)
        r.store(*places)
    emb[...] = (dot(act_three_m[...], four_m[...]) + dot(act_three_o[...], four_o[...])).astype(BF)


def back_kernel(r):
    back_two, back_one_m, back_one_o = r.kept
    back_m, back_o, three_m, three_o, slope_two = r.need(0, 1, 2, 3, 4)

    def go_back(at):
        back_two[:, at] = (
            (dot_bt(back_m[...], three_m[at, :]) + dot_bt(back_o[...], three_o[at, :])) * slope_two[:, at]
        ).astype(BF)

    tiles(three_m.shape[0], go_back)
    r.store(0)
    two_o, slope_o, two_m, slope_m = r.need(5, 6, 7, 8)
    for two, slope, back, place in ((two_o, slope_o, back_one_o, 2), (two_m, slope_m, back_one_m, 1)):

        def go_back(at):
            back[:, at] = (dot_bt(back_two[...], two[at, :]) * slope[:, at]).astype(BF)

        tiles(two.shape[0], go_back)
        r.store(place)


def grad_kernel(r, bit):
    left, left_o, right, right_o = r.need(0, 1, 2, 3)
    half = r.kept[0].shape[0]
    for place, of in ((0, 1 - bit[0]), (1, bit[0])):
        out = r.kept[place]

        def grads(at):
            rows = pl.ds(pl.multiple_of(of * half + at.start, min(half, TILE)), at.size)
            out[at, :] = (dot_t(left[:, rows], right[...]) + dot_t(left_o[:, rows], right_o[...])).astype(BF)

        tiles(half, grads)
        r.store(place)


def grads_kernel(r, bit, core):
    left, left_o, right, right_o, three, three_o, cots = r.need(0, 1, 2, 3, 4, 5, 6)
    half, hidden, width = r.kept[0].shape[0], right.shape[1], cots.shape[1]
    rows = right.shape[0]
    cot = cots.at[pl.ds(pl.multiple_of(core[0] * rows, rows), rows), :]
    cot_o = cots.at[pl.ds(pl.multiple_of((1 - core[0]) * rows, rows), rows), :]
    for place, of in ((0, 1 - bit[0]), (1, bit[0])):
        out = r.kept[place]

        def grads(at):
            rows = pl.ds(pl.multiple_of(of * half + at.start, min(half, TILE)), at.size)
            out[at, :hidden] = (dot_t(left[:, rows], right[...]) + dot_t(left_o[:, rows], right_o[...])).astype(BF)
            out[at, hidden : hidden + width] = (
                dot_t(three[:, rows], cot[...]) + dot_t(three_o[:, rows], cot_o[...])
            ).astype(BF)

        tiles(half, grads)
    feats, feats_o, back, back_o = r.need(7, 8, 9, 10)
    units = back.shape[1]
    for place, of in ((0, 1 - bit[0]), (1, bit[0])):
        out = r.kept[place]
        groups = feats.shape[1] // 2 // half
        for g in range(groups):
            lanes = slice(hidden + width + g * units, hidden + width + (g + 1) * units)

            def grads(at):
                rows = pl.ds(pl.multiple_of((of * groups + g) * half + at.start, min(half, TILE)), at.size)
                out[at, lanes] = (dot_t(feats[:, rows], back[...]) + dot_t(feats_o[:, rows], back_o[...])).astype(BF)

            tiles(half, grads)
        r.store(place)


def finish_kernel(factor, r, bit):
    (grad,) = r.kept
    parts = r.need(0, 1)
    half = parts[0].shape[0]
    step = min(half, 64)
    for part, of in zip(parts, (bit[0], 1 - bit[0])):

        def chunk(j, carry):
            at = pl.ds(pl.multiple_of(j * step, step), step)
            to = pl.ds(pl.multiple_of(of * half + j * step, step), step)
            grad[to, :] = part[at, :].astype(F32) * factor
            return carry

        lax.fori_loop(0, half // step, chunk, 0)


def finish_side_kernel(factor, r, bit):
    one, two, four = r.kept
    parts = r.need(0, 1)
    half = parts[0].shape[0]
    step = min(half, 64)
    hidden, width, units = two.shape[1], four.shape[1], one.shape[1]
    groups = one.shape[0] // 2 // half
    for part, of in zip(parts, (bit[0], 1 - bit[0])):

        def chunk(j, carry):
            at = pl.ds(pl.multiple_of(j * step, step), step)
            for g in range(groups):
                to = pl.ds(pl.multiple_of((of * groups + g) * half + j * step, step), step)
                lanes = slice(hidden + width + g * units, hidden + width + (g + 1) * units)
                one[to, :] = part[at, lanes].astype(F32) * factor
            return carry

        lax.fori_loop(0, half // step, chunk, 0)
    r.store(0)
    for part, of in zip(parts, (bit[0], 1 - bit[0])):

        def chunk(j, carry):
            at = pl.ds(pl.multiple_of(j * step, step), step)
            to = pl.ds(pl.multiple_of(of * half + j * step, step), step)
            two[to, :] = part[at, :hidden].astype(F32) * factor
            four[to, :] = part[at, hidden : hidden + width].astype(F32) * factor
            return carry

        lax.fori_loop(0, half // step, chunk, 0)


def pack_kernel(peers_of, r, place, counts, core):
    rows, cots = r.need(0, 1)
    (pack,) = r.kept
    slots, width = cots.shape[1:]
    span = slots // 2
    base = 1 << 7
    begin = pl.multiple_of(core[0] * span, span)
    slot = lax.broadcasted_iota(jnp.int32, (span, width), 0) + begin
    line = lax.broadcasted_iota(jnp.int32, (8, slots), 0)
    lane = lax.broadcasted_iota(jnp.int32, (8, slots), 1)
    peers = peers_of(place, core[0])
    pack[:, span:, :] = jnp.zeros((pack.shape[0], 8, width), BF)
    for k in range(pack.shape[0]):
        peer = peers(k)
        count = counts[peer]
        block = cots[peer, pl.ds(begin, span), :].astype(F32)
        pack[k, :span, :] = jnp.where(slot < count, block, 0.0).astype(BF)
        row = jnp.where(lane < count, jnp.broadcast_to(rows[pl.ds(peer, 1), :], line.shape), 0)
        digits = jnp.where(line == 0, row // base, jnp.where(line == 1, row % base, 0))
        pack[k, span:, :slots] = digits.astype(F32).astype(BF)


def hot_kernel(there, r, rows, core, rows_f32, cots):
    mine, other, _ = r.need(0, 1, 2)
    fetched, table = r.kept
    peers, span = fetched.shape[0], fetched.shape[1]
    begin = core[0] * span
    cots[core[0]] = mine[:, :span, :].astype(F32) * learn_rate
    cots[1 - core[0]] = other[:, :span, :].astype(F32) * learn_rate

    def fetch(k, carry):
        for j in range(span):
            rows_f32[k, pl.ds(j, 1), :] = table[pl.ds(rows[k * 2 * span + begin + j], 1), :]
        return carry

    lax.fori_loop(0, peers, fetch, 0)
    fetched[...] = rows_f32[...].astype(BF)
    r.store(0)

    for k in range(peers):
        own = jnp.where(core[0] == 0, k, there[k])
        for half, block in ((0, k), (1, there[k])):
            for j in range(span):
                at = pl.ds(rows[own * 2 * span + half * span + j], 1)
                table[at, :] = table[at, :] - cots[half, block, pl.ds(j, 1), :]


def unpack_kernel(peers_of, r, place, counts, core):
    mine, other = r.need(0, 1)
    (emb,) = r.kept
    span = mine.shape[1]
    line = lax.broadcasted_iota(jnp.int32, mine.shape[1:], 0)
    for source, half in ((mine, core[0]), (other, 1 - core[0])):
        peers = peers_of(place, half)
        for k in range(mine.shape[0]):
            peer = peers(k)
            count = counts[peer]
            begin = pl.multiple_of(half * span, span)
            block = jnp.where(line + begin < count, source[k].astype(F32), 0.0)
            emb[peer, pl.ds(begin, span), :] = block.astype(BF)


def swap(x):
    return lax.ppermute(x, "mp", [(0, 1), (1, 0)])


def in_order(mine, other, core, axis):
    first = jnp.where(core == 0, mine, other)
    second = jnp.where(core == 0, other, mine)
    return jnp.concatenate([first, second], axis=axis)


def as_rows(blocks, lanes):
    number, rows, width = blocks.shape
    across = lanes // width
    down = -(-number // across)
    blocks = jnp.pad(blocks, ((0, down * across - number), (0, 0), (0, 0)))
    return blocks.reshape(down, across, rows, width).transpose(0, 2, 1, 3).reshape(down * rows, lanes)


def as_blocks(rows, shape):
    number, height, width = shape
    across = rows.shape[1] // width
    blocks = rows.reshape(-1, height, across, width).transpose(0, 2, 1, 3)
    return blocks.reshape(-1, height, width)[:number]


def make_reduce(count, hops):
    steps = len(hops)

    def order_for(name):
        first, second, third = hops[:3]
        other = [second, first, third] if name == "three" else [third, first, second]
        return [hops, other + hops[3:]]

    def bit_of(name, s):
        order = order_for(name)
        core = lax.axis_index("mp")
        place = lax.axis_index("dp")
        dual = jnp.where(core == 0, order[0][s][1], order[1][s][1])
        return lax.population_count(place & dual) & 1

    def reduce(sent, kept, name, rider=None, turn=None, halvings=3):
        blocks = [rider]
        order = order_for(name)

        def exchange(x, s, kind):
            pairs = [
                (i * 2 + c, (i ^ order[c][s][0]) * 2 + c) for i in range(count) for c in range(2)
            ]
            rows = x.shape[0]
            if blocks[0] is None:
                return lax.ppermute(x, ("dp", "mp"), pairs)
            block = blocks[0].shape[1:]
            split = blocks[0].reshape((-1, 2, 1 << s) + block)
            leaving = split[:, 1].reshape((-1,) + block)
            x = leaving if kind == "home" else jnp.concatenate([x, as_rows(leaving, x.shape[1])], axis=0)
            came = lax.ppermute(x, ("dp", "mp"), pairs)
            joining = came if kind == "home" else as_blocks(came[rows:], leaving.shape)
            joining = joining.reshape(split[:, 1].shape)
            blocks[0] = jnp.stack([split[:, 0], joining], axis=1).reshape((-1,) + block)
            return came[:rows] if kind != "full" or s else came

        def bit(s):
            return bit_of(name, s)

        def total(terms, shift, size):
            return sum(lax.dynamic_slice_in_dim(t, at + shift, size, 0).astype(F32) for t, at in terms)

        terms = [(kept, 0), (exchange(sent, 0, "half"), 0)]
        size = kept.shape[0]
        for s in range(1, halvings):
            size //= 2
            b = bit(s)
            came = exchange(total(terms, (1 - b) * size, size).astype(BF), s, "half")
            terms = [(t, at + b * size) for t, at in terms] + [(came, 0)]
        mine = total(terms, 0, size).astype(BF)
        for s in range(halvings, steps):
            mine = (mine.astype(F32) + exchange(mine, s, "both").astype(F32)).astype(BF)
        if turn is not None:
            blocks[0] = turn(blocks[0])
            for s in range(halvings, steps):
                exchange(blocks[0], s, "home")
        for s in reversed(range(1, halvings)):
            came = exchange(mine, s, "full")
            b = bit(s)
            mine = jnp.concatenate([jnp.where(b == 0, mine, came), jnp.where(b == 0, came, mine)], axis=0)
        came = exchange(mine, 0, "full")
        return (mine, came), blocks[0]

    def combos_of(core):
        combos = [0]
        for mask, _ in order_for("three")[core]:
            combos += [c ^ mask for c in combos]
        return combos

    return reduce, bit_of, combos_of


def make_local(count, hops):
    reduce, bit_of, combos_of = make_reduce(count, hops)
    combos = [combos_of(0), combos_of(1)]
    there = [combos[1].index(c) for c in combos[0]]

    def local(
        hot_rows,
        hot_count,
        hot_cot,
        table,
        cold_ids,
        hash_mult,
        hash_add,
        layer_one,
        layer_two,
        layer_three,
        layer_four,
        cold_cot,
    ):
        core = lax.axis_index("mp")
        place = lax.axis_index("dp")
        width = table.shape[1]
        one_o, two_o, three_o, four_o = swap(layer_one), swap(layer_two), swap(layer_three), swap(layer_four)

        number = cold_ids.shape[0] // 2
        depth, half = layer_one.shape
        hidden = layer_two.shape[1]
        unit = 2 * number * half * depth
        feats, act_one_m, slope_one_m = call(
            first_kernel,
            [((number, depth), BF), ((number, half), BF), ((number, half), F32)],
            [cold_ids[:, None], hash_mult[None, :], hash_add[None, :], layer_one],
            scalars=[core],
            flops=unit * 2,
        )
        feats_p = swap(feats)
        act_one_o, slope_one_o, act_two, slope_two, emb, back_three_m, back_three_o, act_three_m, act_three_o = call(
            second_kernel,
            [
                ((number, half), BF), ((number, half), F32), ((number, hidden), BF), ((number, hidden), F32),
                ((number, width), BF), ((number, half), BF), ((number, half), BF), ((number, half), BF),
                ((number, half), BF),
            ],
            [feats, one_o, act_one_m, layer_two, two_o, layer_three, three_o, layer_four, four_o, cold_cot],
            [((number, half), F32)] * 2,
            scalars=[core],
            flops=unit * 6,
        )
        act_two_p, back_three_p = swap(act_two), swap(back_three_o)
        act_three_p, act_one_p = swap(act_three_o), swap(act_one_o)
        back_two, back_one_m, back_one_o = call(
            back_kernel,
            [((number, hidden), BF), ((number, half), BF), ((number, half), BF)],
            [
                back_three_m, back_three_o, layer_three, three_o, slope_two, two_o, slope_one_o, layer_two, slope_one_m,
            ],
            flops=unit * 4,
        )
        back_two_p, back_one_p = swap(back_two), swap(back_one_o)
        cold_emb = in_order(emb, swap(emb), core, 0)
        factor = float(cold_ids.shape[0] * count) ** (-0.5)
        slots = hot_rows.shape[2]
        span = slots // 2

        def peers_of(place, core):
            return lambda k: place[0] ^ jnp.where(core == 0, combos[0][k], combos[1][k])

        (pack,) = call(
            functools.partial(pack_kernel, peers_of),
            [((count, span + 8, width), BF)],
            [hot_rows[0], hot_cot[0]],
            scalars=[place, hot_count[0], core],
        )
        sent, kept = call(
            grad_kernel,
            [((hidden // 2, half), BF)] * 2,
            [act_two, act_two_p, back_three_m, back_three_p],
            scalars=[bit_of("three", 0)],
            flops=unit * 2,
        )
        updated = []

        def turn(pack):
            digits = pack[:, span : span + 2, :slots].astype(F32).astype(jnp.int32)
            wanted = (digits[:, 0] * 128 + digits[:, 1]).reshape(-1)
            other_pack = swap(pack)
            fetched, new_table = call(
                functools.partial(hot_kernel, there),
                [((count, span, width), BF), (table.shape, F32)],
                [pack, other_pack, table],
                [((count, span, width), F32), ((2, count, span, width), F32)],
                scalars=[wanted, core],
                shared=[(2, 1)],
            )
            updated.append(new_table)
            return fetched

        halves, returned = reduce(sent, kept, "three", pack, turn)
        (new_table,) = updated
        (grad_three,) = call(
            functools.partial(finish_kernel, factor), [((hidden, half), F32)], halves, scalars=[bit_of("three", 0)]
        )
        sent, kept = call(
            grads_kernel,
            [((half // 2, hidden + width + depth), BF)] * 2,
            [
                act_one_m, act_one_p, back_two, back_two_p, act_three_m, act_three_p, cold_cot,
                feats, feats_p, back_one_m, back_one_p,
            ],
            scalars=[bit_of("one", 0), core],
            flops=unit * 4,
        )
        halves, _ = reduce(sent, kept, "one")
        grad_one, grad_two, grad_four = call(
            functools.partial(finish_side_kernel, factor),
            [((depth, half), F32), ((half, hidden), F32), ((half, width), F32)],
            halves,
            scalars=[bit_of("one", 0)],
        )

        other_returned = swap(returned)
        (hot_emb,) = call(
            functools.partial(unpack_kernel, peers_of),
            [((count, slots, width), BF)],
            [returned, other_returned],
            scalars=[place, hot_count[0], core],
        )
        hot_emb = hot_emb[None]
        return hot_emb, new_table, cold_emb, grad_one, grad_two, grad_three, grad_four

    return local


def solution(mesh):
    in_specs = (
        P("dp", None, None),
        P("dp", None),
        P("dp", None, None, None),
        P("dp", None),
        P("dp"),
        P(),
        P(),
        P(None, "mp"),
        P("mp", None),
        P(None, "mp"),
        P("mp", None),
        P("dp", None),
    )
    out_specs = (
        P("dp", None, None, None),
        P("dp", None),
        P("dp", None),
        P(None, "mp"),
        P("mp", None),
        P(None, "mp"),
        P("mp", None),
    )
    local = make_local(mesh.shape["dp"], hops_of(mesh))

    return jax.shard_map(local, mesh=mesh, in_specs=in_specs, out_specs=out_specs, check_vma=False)
```

profile of v0, /device:TPU:0, one launch (start us, length us, event | category | flops | bytes accessed | tf_op | source)
XLA Modules:
  0.0 165.0 jit_solution(7771040491269145684)
XLA Ops:
  0.6 0.6 collective-permute-start
  1.3 0.4 collective-permute-start.2
  1.8 1.7 %copy.19.refs_1_ = s32[1024,1]{1,0:T(8,128)} copy(s32[1024,1]{0,1:T(1,128)} %bitcast.158) | data formatting | bytes 8192 | tf_op jit(solution)/shard_map/broadcast_in_dim | solution.py:506
  3.5 5.1 %shard_map.172 = (bf16[512,1024]{1,0:T(8,128)(2,1)}, bf16[512,512]{1,0:T(8,128)(2,1)}, f32[512,512]{1,0:T(8,128)}) custom-call(s32[1]{0:T(128)} %bitcast.2.refs_2_.refs_0_.refs_1_, s32[1024,1]{1,0:T(8,128)} %copy.19.refs_1_, s32[1,1024]{1,0:T(1,128)} %bitcast.161, s32[1,1024]{1,0:T(1,128)} %bitcast.162, bf16[1024,512]{1,0:T(8,128)(2,1)} %refs_4_.3), custom_call_target="tpu_custom_call" | custom-call | flops 1073741824 | bytes 3682304 | tf_op jit(solution)/shard_map/pallas_call | solution.py:123
  8.6 0.6 copy-done.15
  9.2 0.4 copy-done.12
  9.6 0.4 copy-done.3
  9.9 0.3 copy-done.4
  10.3 7.1 %shard_map.173 = (bf16[512,512]{1,0:T(8,128)(2,1)}, f32[512,512]{1,0:T(8,128)}, bf16[512,1024]{1,0:T(8,128)(2,1)}, f32[512,1024]{1,0:T(8,128)}, bf16[512,128]{1,...) custom-call(s32[1]{0:T(128)} %bitcast.2.refs_2_.refs_0_.refs_1_, ...), custom_call_target="tpu_custom_call" | custom-call | flops 3221225472 | bytes 14286848 | tf_op jit(solution)/shard_map/pallas_call | solution.py:123
  17.4 0.5 collective-permute-start.4
  18.0 0.4 collective-permute-start.20
  18.4 2.3 %shard_map.171 = bf16[16,24,128]{2,1,0:T(8,128)(2,1)} custom-call(s32[1]{0:T(128)} %bitcast.refs_0_, s32[16]{0:T(128)} %bitcast.159, s32[1]{0:T(128)} %bitcast.2.refs_2_.refs_0_.refs_1_, s32[16,32]{1,0:T(8,128)} %bitcast.157, bf16[16,32,128]{2,1,0:T(8,128)(2,1)} %bitcast.144), custom_call_target="tpu_custom_call" | custom-call | bytes 231424 | tf_op jit(solution)/shard_map/pallas_call | solution.py:123
  20.7 0.8 fusion.6
  21.7 0.8 copy-done.14
  22.4 0.3 copy-done.13
  22.8 4.0 %shard_map.174 = (bf16[512,512]{1,0:T(8,128)(2,1)}, bf16[512,512]{1,0:T(8,128)(2,1)}) custom-call(s32[1]{0:T(128)} %bitcast.7.refs_0_, bf16[512,1024]{1,0:T(8,128)(2,1)} %get-tuple-element.33.refs_1_, bf16[512,1024]{1,0:T(8,128)(2,1)} %copy-done.13, bf16[512,512]{1,0:T(8,128)(2,1)} %get-tuple-element.34.refs_3_.refs_0_, bf16[512,512]{1,0:T(8,128)(2,1)} %copy-done.14), custom_call_target="tpu_custom_call" | custom-call | flops 1073741824 | bytes 4194304 | tf_op jit(solution)/shard_map/pallas_call | solution.py:123
  26.8 1.1 pad_maximum_fusion.1
  27.9 2.6 %collective-permute-start.6 = (bf16[560,512]{1,0:T(8,128)(2,1)S(1)}, bf16[560,512]{1,0:T(8,128)(2,1)S(1)}, u32[]{:S(2)}, u32[]{:S(2)}) collective-permute-start(bf16[560,512]{1,0:T(8,128)(2,1)S(1)} %pad_maximum_fusion.1), channel_id=1, source_target_pairs={{0,2},{1,5},{2,0},{3,7},{4,6},{5,1},{6,4},{7,3},{8,10},{9,13},{10,... | collective-permute-start | bytes 1720328 | tf_op jit(solution)/shard_map/ppermute | solution.py:433
  30.5 6.3 %shard_map.177 = (bf16[512,1024]{1,0:T(8,128)(2,1)}, bf16[512,512]{1,0:T(8,128)(2,1)}, bf16[512,512]{1,0:T(8,128)(2,1)}) custom-call(bf16[512,512]{1,0:T(8,128)(2,1)} %get-tuple-element.34.refs_3_.refs_0_, bf16[512,512]{1,0:T(8,128)(2,1)} %get-tuple-element.35.refs_1_, bf16[1024,512]{1,0:T(8,128)(2,1)} %refs_2_.1, bf16[1024,512]{1,0:T(8,128)(2,1)} %copy-done.4, ...), custom_call_target="tpu_custom_call" | custom-call | flops 2147483648 | bytes 11534336 | tf_op jit(solution)/shard_map/pallas_call | solution.py:123
  36.8 0.2 collective-permute-start.18
  37.0 0.3 collective-permute-start.21
  37.5 0.7 collective-permute-done.6
  38.5 2.1 %collective-permute-start.7 = (bf16[304,512]{1,0:T(8,128)(2,1)S(1)}, bf16[304,512]{1,0:T(8,128)(2,1)S(1)}, u32[]{:S(2)}, u32[]{:S(2)}) collective-permute-start(bf16[304,512]{1,0:T(8,128)(2,1)S(1)} %pad_maximum_fusion.5), channel_id=1, source_target_pairs={{0,4},{1,3},{2,6},{3,1},{4,0},{5,7},{6,2},{7,5},{8,12},{9,11},{10,... | collective-permute-start | bytes 933896 | tf_op jit(solution)/shard_map/ppermute | solution.py:433
  40.6 0.7 collective-permute-done.17.refs_3_
  41.3 0.7 collective-permute-done.19.refs_7_
  42.1 6.2 %shard_map.178 = (bf16[256,2176]{1,0:T(8,128)(2,1)}, bf16[256,2176]{1,0:T(8,128)(2,1)}) custom-call(s32[1]{0:T(128)} %bitcast.51.refs_0_, s32[1]{0:T(128)} %bitcast.2.refs_2_.refs_0_.refs_1_, bf16[512,512]{1,0:T(8,128)(2,1)} %get-tuple-element.32.refs_3_.refs_2_, bf16[512,512]{1,0:T(8,128)(2,1)} %collective-permute-done.17.refs_3_, ...), custom_call_target="tpu_custom_call" | custom-call | flops 2147483648 | bytes 9830400 | tf_op jit(solution)/shard_map/pallas_call | solution.py:123
  48.3 1.3 collective-permute-start.22
  49.9 1.6 collective-permute-start.8
  51.6 5.8 %collective-permute-done.8 = bf16[176,512]{1,0:T(8,128)(2,1)S(1)} collective-permute-done((bf16[176,512]{1,0:T(8,128)(2,1)S(1)}, bf16[176,512]{1,0:T(8,128)(2,1)S(1)}, u32[]{:S(2)}, u32[]{:S(2)}) %collective-permute-start.8) | collective-permute-done | bytes 180256 | tf_op jit(solution)/shard_map/ppermute | solution.py:433
  57.5 1.0 add_convert_fusion.6
  58.6 3.7 %collective-permute-start.9 = (bf16[176,512]{1,0:T(8,128)(2,1)S(1)}, bf16[176,512]{1,0:T(8,128)(2,1)S(1)}, u32[]{:S(2)}, u32[]{:S(2)}) collective-permute-start(bf16[176,512]{1,0:T(8,128)(2,1)S(1)} %pad_maximum_fusion.10), channel_id=1, source_target_pairs={{0,24},{1,25},{2,26},{3,27},{4,28},{5,29},{6,30},{7,31},{8,16},{9,... | collective-permute-start | bytes 540680 | tf_op jit(solution)/shard_map/ppermute | solution.py:433
  62.2 1.8 %collective-permute-done.22 = bf16[256,2176]{1,0:T(8,128)(2,1)S(1)} collective-permute-done((bf16[256,2176]{1,0:T(8,128)(2,1)}, bf16[256,2176]{1,0:T(8,128)(2,1)S(1)}, u32[]{:S(2)}, u32[]{:S(2)}) %collective-permute-start.22) | collective-permute-done | bytes 1114144 | tf_op jit(solution)/shard_map/ppermute | solution.py:428
  64.2 1.6 collective-permute-start.23
  65.8 2.1 %collective-permute-done.9 = bf16[176,512]{1,0:T(8,128)(2,1)S(1)} collective-permute-done((bf16[176,512]{1,0:T(8,128)(2,1)S(1)}, bf16[176,512]{1,0:T(8,128)(2,1)S(1)}, u32[]{:S(2)}, u32[]{:S(2)}) %collective-permute-start.9) | collective-permute-done | bytes 180256 | tf_op jit(solution)/shard_map/ppermute | solution.py:433
  67.9 9.0 %collective-permute-start.10 = (bf16[16,24,128]{2,1,0:T(8,128)(2,1)S(1)}, bf16[16,24,128]{2,1,0:T(8,128)(2,1)S(1)}, u32[]{:S(2)}, u32[]{:S(2)}) collective-permute-start(bf16[16,24,128]{2,1,0:T(8,128)(2,1)S(1)} %bitcast.116), channel_id=1, source_target_pairs={{0,1},{1,0},{2,3},{3,2},{4,5},{5,4},{6,7},{7,6},{8,9},{9,8},{10,11... | collective-permute-start | bytes 294920 | tf_op jit(solution)/shard_map/ppermute | solution.py:379
  77.0 0.7 add.115.refs_0_
  77.7 0.3 collective-permute-done.10.refs_3_
  77.9 0.6 copy-done.10
  78.6 6.7 %shard_map.175 = (bf16[16,16,128]{2,1,0:T(8,128)(2,1)}, f32[4096,128]{1,0:T(8,128)}) custom-call(s32[512]{0:T(512)} %add.115.refs_0_, s32[1]{0:T(128)} %bitcast.2.refs_2_.refs_0_.refs_1_, bf16[16,24,128]{2,1,0:T(8,128)(2,1)} %bitcast.117, bf16[16,24,128]{2,1,0:T(8,128)(2,1)} %copy-done.10, f32[4096,128]{1,0:T(8,128)} %refs_4_.5), custom_call_target="tpu_custom_call" | custom-call | bytes 4456448 | tf_op jit(solution)/shard_map/pallas_call | solution.py:123
  85.2 0.8 fusion.8
  86.0 3.4 %collective-permute-start.11 = (bf16[8,16,128]{2,1,0:T(8,128)(2,1)S(1)}, bf16[8,16,128]{2,1,0:T(8,128)(2,1)S(1)}, u32[]{:S(2)}, u32[]{:S(2)}) collective-permute-start(bf16[8,16,128]{2,1,0:T(8,128)(2,1)S(1)} %get-tuple-element.80), channel_id=1, source_target_pairs={{0,24},{1,25},{2,26},{3,27},{4,28},{5,29},{6,30},{7,31},{8,16},{9,... | collective-permute-start | bytes 98312 | tf_op jit(solution)/shard_map/ppermute | solution.py:433
  89.5 2.2 %collective-permute-done.11 = bf16[8,16,128]{2,1,0:T(8,128)(2,1)S(1)} collective-permute-done((bf16[8,16,128]{2,1,0:T(8,128)(2,1)S(1)}, bf16[8,16,128]{2,1,0:T(8,128)(2,1)S(1)}, u32[]{:S(2)}, u32[]{:S(2)}) %collective-permute-start.11) | collective-permute-done | bytes 32800 | tf_op jit(solution)/shard_map/ppermute | solution.py:433
  91.8 1.1 add_convert_fusion.3
  93.1 2.0 %collective-permute-start.12 = (bf16[160,512]{1,0:T(8,128)(2,1)S(1)}, bf16[160,512]{1,0:T(8,128)(2,1)S(1)}, u32[]{:S(2)}, u32[]{:S(2)}) collective-permute-start(bf16[160,512]{1,0:T(8,128)(2,1)S(1)} %pad_maximum_fusion.11), channel_id=1, source_target_pairs={{0,8},{1,9},{2,10},{3,11},{4,12},{5,13},{6,14},{7,15},{8,0},{9,1},... | collective-permute-start | bytes 491528 | tf_op jit(solution)/shard_map/ppermute | solution.py:433
  95.0 7.5 %collective-permute-done.12 = bf16[160,512]{1,0:T(8,128)(2,1)S(1)} collective-permute-done((bf16[160,512]{1,0:T(8,128)(2,1)S(1)}, bf16[160,512]{1,0:T(8,128)(2,1)S(1)}, u32[]{:S(2)}, u32[]{:S(2)}) %collective-permute-start.12) | collective-permute-done | bytes 163872 | tf_op jit(solution)/shard_map/ppermute | solution.py:433
  102.5 1.1 add_convert_fusion.2
  103.6 3.5 %collective-permute-start.25 = (bf16[64,2176]{1,0:T(8,128)(2,1)S(1)}, bf16[64,2176]{1,0:T(8,128)(2,1)S(1)}, u32[]{:S(2)}, u32[]{:S(2)}) collective-permute-start(bf16[64,2176]{1,0:T(8,128)(2,1)S(1)} %add_convert_fusion.2), channel_id=1, source_target_pairs={{0,24},{1,25},{2,26},{3,27},{4,28},{5,29},{6,30},{7,31},{8,16},{9,... | collective-permute-start | bytes 835592 | tf_op jit(solution)/shard_map/ppermute | solution.py:428
  107.2 4.9 %collective-permute-done.25 = bf16[64,2176]{1,0:T(8,128)(2,1)S(1)} collective-permute-done((bf16[64,2176]{1,0:T(8,128)(2,1)S(1)}, bf16[64,2176]{1,0:T(8,128)(2,1)S(1)}, u32[]{:S(2)}, u32[]{:S(2)}) %collective-permute-start.25) | collective-permute-done | bytes 278560 | tf_op jit(solution)/shard_map/ppermute | solution.py:428
  112.2 4.2 %collective-permute-start.26 = (bf16[64,2176]{1,0:T(8,128)(2,1)S(1)}, bf16[64,2176]{1,0:T(8,128)(2,1)S(1)}, u32[]{:S(2)}, u32[]{:S(2)}) collective-permute-start(bf16[64,2176]{1,0:T(8,128)(2,1)S(1)} %add_convert_fusion.1), channel_id=1, source_target_pairs={{0,8},{1,5},{2,10},{3,7},{4,12},{5,1},{6,14},{7,3},{8,0},{9,13},{1... | collective-permute-start | bytes 835592 | tf_op jit(solution)/shard_map/ppermute | solution.py:428
  116.5 4.4 %collective-permute-done.26 = bf16[64,2176]{1,0:T(8,128)(2,1)S(1)} collective-permute-done((bf16[64,2176]{1,0:T(8,128)(2,1)S(1)}, bf16[64,2176]{1,0:T(8,128)(2,1)S(1)}, u32[]{:S(2)}, u32[]{:S(2)}) %collective-permute-start.26) | collective-permute-done | bytes 278560 | tf_op jit(solution)/shard_map/ppermute | solution.py:428
  121.1 2.1 %collective-permute-done.13 = bf16[288,512]{1,0:T(8,128)(2,1)S(1)} collective-permute-done((bf16[288,512]{1,0:T(8,128)(2,1)S(1)}, bf16[288,512]{1,0:T(8,128)(2,1)S(1)}, u32[]{:S(2)}, u32[]{:S(2)}) %collective-permute-start.13) | collective-permute-done | bytes 294944 | tf_op jit(solution)/shard_map/ppermute | solution.py:433
  123.3 7.3 %collective-permute-done.27 = bf16[128,2176]{1,0:T(8,128)(2,1)S(1)} collective-permute-done((bf16[128,2176]{1,0:T(8,128)(2,1)S(1)}, bf16[128,2176]{1,0:T(8,128)(2,1)S(1)}, u32[]{:S(2)}, u32[]{:S(2)}) %collective-permute-start.27) | collective-permute-done | bytes 557088 | tf_op jit(solution)/shard_map/ppermute | solution.py:428
  130.9 0.2 collective-permute-start.28
  131.2 2.0 %collective-permute-start.14 = (bf16[544,512]{1,0:T(8,128)(2,1)S(1)}, bf16[544,512]{1,0:T(8,128)(2,1)S(1)}, u32[]{:S(2)}, u32[]{:S(2)}) collective-permute-start(bf16[544,512]{1,0:T(8,128)(2,1)S(1)} %pad_maximum_fusion.2), channel_id=1, source_target_pairs={{0,2},{1,5},{2,0},{3,7},{4,6},{5,1},{6,4},{7,3},{8,10},{9,13},{10,... | collective-permute-start | bytes 1671176 | tf_op jit(solution)/shard_map/ppermute | solution.py:433
  133.2 1.3 collective-permute-done.16
  134.6 0.7 pad_maximum_fusion.8
  135.3 17.1 %collective-permute-done.14.refs_2_ = bf16[544,512]{1,0:T(8,128)(2,1)S(1)} collective-permute-done((bf16[544,512]{1,0:T(8,128)(2,1)S(1)}, bf16[544,512]{1,0:T(8,128)(2,1)S(1)}, u32[]{:S(2)}, u32[]{:S(2)}) %collective-permute-start.14) | collective-permute-done | bytes 557088 | tf_op jit(solution)/shard_map/ppermute | solution.py:433
  152.4 0.8 copy-done.5
  153.4 0.8 pad_maximum_fusion.4.refs_1_
  154.2 2.8 %shard_map.180 = f32[1024,512]{1,0:T(8,128)} custom-call(s32[1]{0:T(128)} %bitcast.7.refs_0_, bf16[512,512]{1,0:T(8,128)(2,1)} %pad_maximum_fusion.4.refs_1_, bf16[544,512]{1,0:T(8,128)(2,1)} %copy-done.5), custom_call_target="tpu_custom_call" | custom-call | bytes 3178496 | tf_op jit(solution)/shard_map/pallas_call | solution.py:123
  157.0 0.6 copy-done.11
  157.7 2.3 %shard_map.176 = bf16[16,32,128]{2,1,0:T(8,128)(2,1)} custom-call(s32[1]{0:T(128)} %bitcast.refs_0_, s32[16]{0:T(128)} %bitcast.160, s32[1]{0:T(128)} %bitcast.2.refs_2_.refs_0_.refs_1_, bf16[16,16,128]{2,1,0:T(8,128)(2,1)} %bitcast.124, bf16[16,16,128]{2,1,0:T(8,128)(2,1)} %copy-done.11), custom_call_target="tpu_custom_call" | custom-call | bytes 262144 | tf_op jit(solution)/shard_map/pallas_call | solution.py:123
  160.0 1.0 copy-done.2
  161.0 3.9 %shard_map.179 = (f32[1024,512]{1,0:T(8,128)}, f32[512,1024]{1,0:T(8,128)}, f32[512,128]{1,0:T(8,128)}) custom-call(s32[1]{0:T(128)} %bitcast.51.refs_0_, bf16[256,2176]{1,0:T(8,128)(2,1)} %copy-done, bf16[256,2176]{1,0:T(8,128)(2,1)} %copy-done.2), custom_call_target="tpu_custom_call" | custom-call | bytes 6684672 | tf_op jit(solution)/shard_map/pallas_call | solution.py:123
  (118 shorter events, 2.6 us)
Async XLA Ops:
  0.6 8.0 %collective-permute-start = (bf16[1024,512]{1,0:T(8,128)(2,1)}, bf16[1024,512]{1,0:T(8,128)(2,1)S(1)}, u32[]{:S(2)}, u32[]{:S(2)}) collective-permute-start(bf16[1024,512]{1,0:T(8,128)(2,1)} %refs_4_.3), channel_id=1, source_target_pairs={{0,1},{1,0},{2,3},{3,2},{4,5},{5,4},{6,7},{7,6},{8,9},{9,8},{10,11... | collective-permute-start | bytes 3145736 | tf_op jit(solution)/shard_map/ppermute | solution.py:379
  1.2 7.4 %collective-permute-start.1 = (bf16[512,1024]{1,0:T(8,128)(2,1)}, bf16[512,1024]{1,0:T(8,128)(2,1)S(1)}, u32[]{:S(2)}, u32[]{:S(2)}) collective-permute-start(bf16[512,1024]{1,0:T(8,128)(2,1)} %refs_7_.1), channel_id=1, source_target_pairs={{0,1},{1,0},{2,3},{3,2},{4,5},{5,4},{6,7},{7,6},{8,9},{9,8},{10,11... | collective-permute-start | bytes 3145736 | tf_op jit(solution)/shard_map/ppermute | solution.py:379
  1.3 7.4 %collective-permute-start.2 = (bf16[1024,512]{1,0:T(8,128)(2,1)}, bf16[1024,512]{1,0:T(8,128)(2,1)S(1)}, u32[]{:S(2)}, u32[]{:S(2)}) collective-permute-start(bf16[1024,512]{1,0:T(8,128)(2,1)} %refs_2_.1), channel_id=1, source_target_pairs={{0,1},{1,0},{2,3},{3,2},{4,5},{5,4},{6,7},{7,6},{8,9},{9,8},{10,11... | collective-permute-start | bytes 3145736 | tf_op jit(solution)/shard_map/ppermute | solution.py:379
  1.7 6.9 %collective-permute-start.3 = (bf16[512,128]{1,0:T(8,128)(2,1)}, bf16[512,128]{1,0:T(8,128)(2,1)S(1)}, u32[]{:S(2)}, u32[]{:S(2)}) collective-permute-start(bf16[512,128]{1,0:T(8,128)(2,1)} %refs_8_.2), channel_id=1, source_target_pairs={{0,1},{1,0},{2,3},{3,2},{4,5},{5,4},{6,7},{7,6},{8,9},{9,8},{10,11... | collective-permute-start | bytes 393224 | tf_op jit(solution)/shard_map/ppermute | solution.py:379
  8.6 0.7 copy-start.15
  8.6 1.0 copy-start.12
  8.6 1.3 copy-start.3
  8.6 1.6 copy-start.4
  17.4 4.3 %collective-permute-start.4 = (bf16[512,1024]{1,0:T(8,128)(2,1)}, bf16[512,1024]{1,0:T(8,128)(2,1)S(1)}, u32[]{:S(2)}, u32[]{:S(2)}) collective-permute-start(bf16[512,1024]{1,0:T(8,128)(2,1)} %get-tuple-element.33.refs_1_), channel_id=1, source_target_pairs={{0,1},{1,0},{2,3},{3,2},{4,5},{5,4},{6,7},{7,6},{8,9},{9,8},{10,11... | collective-permute-start | bytes 3145736 | tf_op jit(solution)/shard_map/ppermute | solution.py:379
  17.9 3.7 %collective-permute-start.5 = (bf16[512,512]{1,0:T(8,128)(2,1)}, bf16[512,512]{1,0:T(8,128)(2,1)S(1)}, u32[]{:S(2)}, u32[]{:S(2)}) collective-permute-start(bf16[512,512]{1,0:T(8,128)(2,1)} %get-tuple-element.35.refs_1_), channel_id=1, source_target_pairs={{0,1},{1,0},{2,3},{3,2},{4,5},{5,4},{6,7},{7,6},{8,9},{9,8},{10,11... | collective-permute-start | bytes 1572872 | tf_op jit(solution)/shard_map/ppermute | solution.py:379
  18.0 20.5 %collective-permute-start.20 = (bf16[512,1024]{1,0:T(8,128)(2,1)}, bf16[512,1024]{1,0:T(8,128)(2,1)}, u32[]{:S(2)}, u32[]{:S(2)}) collective-permute-start(bf16[512,1024]{1,0:T(8,128)(2,1)} %get-tuple-element.31.refs_1_.refs_9_), channel_id=1, source_target_pairs={{0,1},{1,0},{2,3},{3,2},{4,5},{5,4},{6,7},{7,6},{8,9},{9,8},{10,11... | collective-permute-start | bytes 3145736 | tf_op jit(solution)/shard_map/ppermute | solution.py:379
  21.6 0.8 copy-start.14
  21.7 1.1 copy-start.13
  27.9 10.3 %collective-permute-start.6 = (bf16[560,512]{1,0:T(8,128)(2,1)S(1)}, bf16[560,512]{1,0:T(8,128)(2,1)S(1)}, u32[]{:S(2)}, u32[]{:S(2)}) collective-permute-start(bf16[560,512]{1,0:T(8,128)(2,1)S(1)} %pad_maximum_fusion.1), channel_id=1, source_target_pairs={{0,2},{1,5},{2,0},{3,7},{4,6},{5,1},{6,4},{7,3},{8,10},{9,13},{10,... | collective-permute-start | bytes 1720328 | tf_op jit(solution)/shard_map/ppermute | solution.py:433
  36.8 1.6 copy-start.6
  36.8 5.3 %collective-permute-start.18 = (bf16[512,1024]{1,0:T(8,128)(2,1)}, bf16[512,1024]{1,0:T(8,128)(2,1)}, u32[]{:S(2)}, u32[]{:S(2)}) collective-permute-start(bf16[512,1024]{1,0:T(8,128)(2,1)} %get-tuple-element.45.refs_4_), channel_id=1, source_target_pairs={{0,1},{1,0},{2,3},{3,2},{4,5},{5,4},{6,7},{7,6},{8,9},{9,8},{10,11... | collective-permute-start | bytes 3145736 | tf_op jit(solution)/shard_map/ppermute | solution.py:379
  37.0 3.6 %collective-permute-start.21 = (bf16[512,512]{1,0:T(8,128)(2,1)}, bf16[512,512]{1,0:T(8,128)(2,1)}, u32[]{:S(2)}, u32[]{:S(2)}) collective-permute-start(bf16[512,512]{1,0:T(8,128)(2,1)} %get-tuple-element.49), channel_id=1, source_target_pairs={{0,1},{1,0},{2,3},{3,2},{4,5},{5,4},{6,7},{7,6},{8,9},{9,8},{10,11... | collective-permute-start | bytes 1572872 | tf_op jit(solution)/shard_map/ppermute | solution.py:379
  37.3 4.0 %collective-permute-start.17 = (bf16[512,512]{1,0:T(8,128)(2,1)}, bf16[512,512]{1,0:T(8,128)(2,1)}, u32[]{:S(2)}, u32[]{:S(2)}) collective-permute-start(bf16[512,512]{1,0:T(8,128)(2,1)} %get-tuple-element.41), channel_id=1, source_target_pairs={{0,1},{1,0},{2,3},{3,2},{4,5},{5,4},{6,7},{7,6},{8,9},{9,8},{10,11... | collective-permute-start | bytes 1572872 | tf_op jit(solution)/shard_map/ppermute | solution.py:379
  38.2 3.9 %collective-permute-start.19 = (bf16[512,512]{1,0:T(8,128)(2,1)}, bf16[512,512]{1,0:T(8,128)(2,1)}, u32[]{:S(2)}, u32[]{:S(2)}) collective-permute-start(bf16[512,512]{1,0:T(8,128)(2,1)} %get-tuple-element.47), channel_id=1, source_target_pairs={{0,1},{1,0},{2,3},{3,2},{4,5},{5,4},{6,7},{7,6},{8,9},{9,8},{10,11... | collective-permute-start | bytes 1572872 | tf_op jit(solution)/shard_map/ppermute | solution.py:379
  38.5 11.2 %collective-permute-start.7 = (bf16[304,512]{1,0:T(8,128)(2,1)S(1)}, bf16[304,512]{1,0:T(8,128)(2,1)S(1)}, u32[]{:S(2)}, u32[]{:S(2)}) collective-permute-start(bf16[304,512]{1,0:T(8,128)(2,1)S(1)} %pad_maximum_fusion.5), channel_id=1, source_target_pairs={{0,4},{1,3},{2,6},{3,1},{4,0},{5,7},{6,2},{7,5},{8,12},{9,11},{10,... | collective-permute-start | bytes 933896 | tf_op jit(solution)/shard_map/ppermute | solution.py:433
  48.3 15.8 %collective-permute-start.22 = (bf16[256,2176]{1,0:T(8,128)(2,1)}, bf16[256,2176]{1,0:T(8,128)(2,1)S(1)}, u32[]{:S(2)}, u32[]{:S(2)}) collective-permute-start(bf16[256,2176]{1,0:T(8,128)(2,1)} %get-tuple-element.51), channel_id=1, source_target_pairs={{0,2},{1,9},{2,0},{3,11},{4,6},{5,13},{6,4},{7,15},{8,10},{9,1},{1... | collective-permute-start | bytes 3342344 | tf_op jit(solution)/shard_map/ppermute | solution.py:428
  49.9 14.2 %copy-start.1 = (bf16[256,2176]{1,0:T(8,128)(2,1)S(1)}, bf16[256,2176]{1,0:T(8,128)(2,1)}, u32[]{:S(2)}) copy-start(bf16[256,2176]{1,0:T(8,128)(2,1)} %get-tuple-element.50) | copy-start | bytes 3342340
  49.9 7.5 %collective-permute-start.8 = (bf16[176,512]{1,0:T(8,128)(2,1)S(1)}, bf16[176,512]{1,0:T(8,128)(2,1)S(1)}, u32[]{:S(2)}, u32[]{:S(2)}) collective-permute-start(bf16[176,512]{1,0:T(8,128)(2,1)S(1)} %pad_maximum_fusion.9), channel_id=1, source_target_pairs={{0,8},{1,9},{2,10},{3,11},{4,12},{5,13},{6,14},{7,15},{8,0},{9,1},... | collective-permute-start | bytes 540680 | tf_op jit(solution)/shard_map/ppermute | solution.py:433
  58.6 9.3 %collective-permute-start.9 = (bf16[176,512]{1,0:T(8,128)(2,1)S(1)}, bf16[176,512]{1,0:T(8,128)(2,1)S(1)}, u32[]{:S(2)}, u32[]{:S(2)}) collective-permute-start(bf16[176,512]{1,0:T(8,128)(2,1)S(1)} %pad_maximum_fusion.10), channel_id=1, source_target_pairs={{0,24},{1,25},{2,26},{3,27},{4,28},{5,29},{6,30},{7,31},{8,16},{9,... | collective-permute-start | bytes 540680 | tf_op jit(solution)/shard_map/ppermute | solution.py:433
  64.2 27.6 %collective-permute-start.23 = (bf16[128,2176]{1,0:T(8,128)(2,1)S(1)}, bf16[128,2176]{1,0:T(8,128)(2,1)}, u32[]{:S(2)}, u32[]{:S(2)}) collective-permute-start(bf16[128,2176]{1,0:T(8,128)(2,1)S(1)} %add_convert_fusion), channel_id=1, source_target_pairs={{0,4},{1,3},{2,6},{3,1},{4,0},{5,7},{6,2},{7,5},{8,12},{9,11},{10,... | collective-permute-start | bytes 1671176 | tf_op jit(solution)/shard_map/ppermute | solution.py:428
  67.9 10.0 %copy-start.7 = (bf16[1,2,8,24,128]{4,3,2,1,0:T(8,128)(2,1)}, bf16[1,2,8,24,128]{4,3,2,1,0:T(8,128)(2,1)S(1)}, u32[]{:S(2)}) copy-start(bf16[1,2,8,24,128]{4,3,2,1,0:T(8,128)(2,1)S(1)} %pad_maximum_fusion.14) | copy-start | bytes 294916
  67.9 10.0 %collective-permute-start.10 = (bf16[16,24,128]{2,1,0:T(8,128)(2,1)S(1)}, bf16[16,24,128]{2,1,0:T(8,128)(2,1)S(1)}, u32[]{:S(2)}, u32[]{:S(2)}) collective-permute-start(bf16[16,24,128]{2,1,0:T(8,128)(2,1)S(1)} %bitcast.116), channel_id=1, source_target_pairs={{0,1},{1,0},{2,3},{3,2},{4,5},{5,4},{6,7},{7,6},{8,9},{9,8},{10,11... | collective-permute-start | bytes 294920 | tf_op jit(solution)/shard_map/ppermute | solution.py:379
  77.9 0.6 copy-start.10
  86.0 5.7 %collective-permute-start.11 = (bf16[8,16,128]{2,1,0:T(8,128)(2,1)S(1)}, bf16[8,16,128]{2,1,0:T(8,128)(2,1)S(1)}, u32[]{:S(2)}, u32[]{:S(2)}) collective-permute-start(bf16[8,16,128]{2,1,0:T(8,128)(2,1)S(1)} %get-tuple-element.80), channel_id=1, source_target_pairs={{0,24},{1,25},{2,26},{3,27},{4,28},{5,29},{6,30},{7,31},{8,16},{9,... | collective-permute-start | bytes 98312 | tf_op jit(solution)/shard_map/ppermute | solution.py:433
  92.9 9.7 %collective-permute-start.24 = (bf16[64,2176]{1,0:T(8,128)(2,1)S(1)}, bf16[64,2176]{1,0:T(8,128)(2,1)S(1)}, u32[]{:S(2)}, u32[]{:S(2)}) collective-permute-start(bf16[64,2176]{1,0:T(8,128)(2,1)S(1)} %add_convert_fusion.3), channel_id=1, source_target_pairs={{0,8},{1,5},{2,10},{3,7},{4,12},{5,1},{6,14},{7,3},{8,0},{9,13},{1... | collective-permute-start | bytes 835592 | tf_op jit(solution)/shard_map/ppermute | solution.py:428
  93.1 9.4 %collective-permute-start.12 = (bf16[160,512]{1,0:T(8,128)(2,1)S(1)}, bf16[160,512]{1,0:T(8,128)(2,1)S(1)}, u32[]{:S(2)}, u32[]{:S(2)}) collective-permute-start(bf16[160,512]{1,0:T(8,128)(2,1)S(1)} %pad_maximum_fusion.11), channel_id=1, source_target_pairs={{0,8},{1,9},{2,10},{3,11},{4,12},{5,13},{6,14},{7,15},{8,0},{9,1},... | collective-permute-start | bytes 491528 | tf_op jit(solution)/shard_map/ppermute | solution.py:433
  103.6 8.5 %collective-permute-start.25 = (bf16[64,2176]{1,0:T(8,128)(2,1)S(1)}, bf16[64,2176]{1,0:T(8,128)(2,1)S(1)}, u32[]{:S(2)}, u32[]{:S(2)}) collective-permute-start(bf16[64,2176]{1,0:T(8,128)(2,1)S(1)} %add_convert_fusion.2), channel_id=1, source_target_pairs={{0,24},{1,25},{2,26},{3,27},{4,28},{5,29},{6,30},{7,31},{8,16},{9,... | collective-permute-start | bytes 835592 | tf_op jit(solution)/shard_map/ppermute | solution.py:428
  112.2 8.7 %collective-permute-start.26 = (bf16[64,2176]{1,0:T(8,128)(2,1)S(1)}, bf16[64,2176]{1,0:T(8,128)(2,1)S(1)}, u32[]{:S(2)}, u32[]{:S(2)}) collective-permute-start(bf16[64,2176]{1,0:T(8,128)(2,1)S(1)} %add_convert_fusion.1), channel_id=1, source_target_pairs={{0,8},{1,5},{2,10},{3,7},{4,12},{5,1},{6,14},{7,3},{8,0},{9,13},{1... | collective-permute-start | bytes 835592 | tf_op jit(solution)/shard_map/ppermute | solution.py:428
  116.4 6.8 %collective-permute-start.13 = (bf16[288,512]{1,0:T(8,128)(2,1)S(1)}, bf16[288,512]{1,0:T(8,128)(2,1)S(1)}, u32[]{:S(2)}, u32[]{:S(2)}) collective-permute-start(bf16[288,512]{1,0:T(8,128)(2,1)S(1)} %pad_maximum_fusion.6), channel_id=1, source_target_pairs={{0,4},{1,3},{2,6},{3,1},{4,0},{5,7},{6,2},{7,5},{8,12},{9,11},{10,... | collective-permute-start | bytes 884744 | tf_op jit(solution)/shard_map/ppermute | solution.py:433
  121.0 9.6 %collective-permute-start.27 = (bf16[128,2176]{1,0:T(8,128)(2,1)S(1)}, bf16[128,2176]{1,0:T(8,128)(2,1)S(1)}, u32[]{:S(2)}, u32[]{:S(2)}) collective-permute-start(bf16[128,2176]{1,0:T(8,128)(2,1)S(1)} %pad_maximum_fusion.3), channel_id=1, source_target_pairs={{0,4},{1,3},{2,6},{3,1},{4,0},{5,7},{6,2},{7,5},{8,12},{9,11},{10,... | collective-permute-start | bytes 1671176 | tf_op jit(solution)/shard_map/ppermute | solution.py:428
  130.9 3.7 %copy-start = (bf16[256,2176]{1,0:T(8,128)(2,1)}, bf16[256,2176]{1,0:T(8,128)(2,1)S(1)}, u32[]{:S(2)}) copy-start(bf16[256,2176]{1,0:T(8,128)(2,1)S(1)} %pad_maximum_fusion.refs_1_) | copy-start | bytes 3342340
  130.9 2.3 %copy-start.9 = (bf16[512,128]{1,0:T(8,128)(2,1)S(1)}, bf16[512,128]{1,0:T(8,128)(2,1)}, u32[]{:S(2)}) copy-start(bf16[512,128]{1,0:T(8,128)(2,1)} %get-tuple-element.40) | copy-start | bytes 393220
  130.9 29.0 %collective-permute-start.28 = (bf16[256,2176]{1,0:T(8,128)(2,1)S(1)}, bf16[256,2176]{1,0:T(8,128)(2,1)S(1)}, u32[]{:S(2)}, u32[]{:S(2)}) collective-permute-start(bf16[256,2176]{1,0:T(8,128)(2,1)S(1)} %pad_maximum_fusion.refs_1_), channel_id=1, source_target_pairs={{0,2},{1,9},{2,0},{3,11},{4,6},{5,13},{6,4},{7,15},{8,10},{9,1},{1... | collective-permute-start | bytes 3342344 | tf_op jit(solution)/shard_map/ppermute | solution.py:428
  131.2 21.2 %collective-permute-start.14 = (bf16[544,512]{1,0:T(8,128)(2,1)S(1)}, bf16[544,512]{1,0:T(8,128)(2,1)S(1)}, u32[]{:S(2)}, u32[]{:S(2)}) collective-permute-start(bf16[544,512]{1,0:T(8,128)(2,1)S(1)} %pad_maximum_fusion.2), channel_id=1, source_target_pairs={{0,2},{1,5},{2,0},{3,7},{4,6},{5,1},{6,4},{7,3},{8,10},{9,13},{10,... | collective-permute-start | bytes 1671176 | tf_op jit(solution)/shard_map/ppermute | solution.py:433
  133.2 1.3 collective-permute-start.16
  152.4 0.8 copy-start.5
  153.3 3.7 %copy-start.8 = (bf16[8,2,1,16,128]{4,3,1,0,2:T(8,128)(2,1)}, bf16[8,2,1,16,128]{4,3,1,0,2:T(8,128)(2,1)S(1)}, u32[]{:S(2)}) copy-start(bf16[8,2,1,16,128]{4,3,1,0,2:T(8,128)(2,1)S(1)} %copy.41) | copy-start | bytes 196612
  153.3 3.7 %collective-permute-start.15 = (bf16[16,16,128]{2,1,0:T(8,128)(2,1)S(1)}, bf16[16,16,128]{2,1,0:T(8,128)(2,1)S(1)}, u32[]{:S(2)}, u32[]{:S(2)}) collective-permute-start(bf16[16,16,128]{2,1,0:T(8,128)(2,1)S(1)} %bitcast.123), channel_id=1, source_target_pairs={{0,1},{1,0},{2,3},{3,2},{4,5},{5,4},{6,7},{7,6},{8,9},{9,8},{10,11... | collective-permute-start | bytes 196616 | tf_op jit(solution)/shard_map/ppermute | solution.py:379
  157.0 0.6 copy-start.11
  160.0 1.0 copy-start.2
where the time goes:
time: 166 us; the launch traced here: 165 us
  waiting for transfers between devices  59.1 us (36%)
  Pallas kernels  46.5 us (28%)
  starting transfers between devices  40.5 us (24%)
  local copies, waits for them, and re-layouts  10.4 us (6%)
  other arithmetic  6.91 us (4%)
    pallas_call x10, Pallas kernels, call(): pl.pallas_call(body, out_shape=shapes, in_specs=[near] * p + [far] * n, o...  46.5 us
    ppermute x8, waiting for transfers between devices, exchange(): came = lax.ppermute(x, ('dp', 'mp'), pairs)  37.5 us
    ppermute x7, waiting for transfers between devices, exchange(): return lax.ppermute(x, ('dp', 'mp'), pairs)  18.5 us
    ppermute x8, starting transfers between devices, exchange(): came = lax.ppermute(x, ('dp', 'mp'), pairs)  17.5 us
    ppermute x14, starting transfers between devices, swap(): return lax.ppermute(x, 'mp', [(0, 1), (1, 0)])  12 us
    ppermute x7, starting transfers between devices, exchange(): return lax.ppermute(x, ('dp', 'mp'), pairs)  11 us
    unnamed x40, local copies, waits for them, and re-layouts  5.94 us
  transfers between devices with their start and end apart: 29, of which 15 were waited for; matrix products, arithmetic and copies ran while one was open for 5% of the time, Pallas kernels for 22%

commit v1 on v0

--- a/solution.py
+++ b/solution.py
@@ -77,7 +77,8 @@
         self.held, self.kept = held, kept
         self.loads = [pltpu.make_async_copy(s, d, load_sems.at[i]) for i, (s, d) in enumerate(zip(inputs, held))]
         self.stores = [pltpu.make_async_copy(s, d, store_sems.at[i]) for i, (s, d) in enumerate(zip(kept, outputs))]
-        self.waited, self.put = set(), set()
+        self.outputs, self.sems = outputs, store_sems
+        self.waited, self.put, self.started = set(), set(), []
         for load in self.loads:
             load.start()
 
@@ -92,11 +93,20 @@
         for i in which:
             self.stores[i].start()
             self.put.add(i)
+            self.started.append(self.stores[i])
+
+    def store_rows(self, i, start, size, again):
+        at = pl.ds(pl.multiple_of(start, size), size)
+        sem = self.sems.at[i + again * len(self.stores)]
+        copy = pltpu.make_async_copy(self.kept[i].at[at, :], self.outputs[i].at[at, :], sem)
+        copy.start()
+        self.put.add(i)
+        self.started.append(copy)
 
     def finish(self):
         self.need(*range(len(self.loads)))
         self.store(*(i for i in range(len(self.stores)) if i not in self.put))
-        for copy in self.stores:
+        for copy in self.started:
             copy.wait()
 
 
@@ -130,7 +140,7 @@
             *(pltpu.VMEM(x.shape, x.dtype) for x in shapes),
             *(pltpu.VMEM(shape, kind) for shape, kind in scratch),
             pltpu.SemaphoreType.DMA((n,)),
-            pltpu.SemaphoreType.DMA((m,)),
+            pltpu.SemaphoreType.DMA((2 * m,)),
         ],
         cost_estimate=pl.CostEstimate(flops=flops, bytes_accessed=moved, transcendentals=0),
     )(*scalars, *args)
@@ -284,12 +294,12 @@
 
 def finish_side_kernel(factor, r, bit):
     one, two, four = r.kept
-    parts = r.need(0, 1)
-    half = parts[0].shape[0]
+    half = r.held[0].shape[0]
     step = min(half, 64)
     hidden, width, units = two.shape[1], four.shape[1], one.shape[1]
     groups = one.shape[0] // 2 // half
-    for part, of in zip(parts, (bit[0], 1 - bit[0])):
+    for again, of in enumerate((bit[0], 1 - bit[0])):
+        (part,) = r.need(again)
 
         def chunk(j, carry):
             at = pl.ds(pl.multiple_of(j * step, step), step)
@@ -300,8 +310,7 @@
             return carry
 
         lax.fori_loop(0, half // step, chunk, 0)
-    r.store(0)
-    for part, of in zip(parts, (bit[0], 1 - bit[0])):
+        r.store_rows(0, of * groups * half, groups * half, again)
 
         def chunk(j, carry):
             at = pl.ds(pl.multiple_of(j * step, step), step)
@@ -311,6 +320,8 @@
             return carry
 
         lax.fori_loop(0, half // step, chunk, 0)
+        r.store_rows(1, of * half, half, again)
+        r.store_rows(2, of * half, half, again)
 
 
 def pack_kernel(peers_of, r, place, counts, core):

time: 166 us -> 165 us (level)
  no operation moved by 1% of the time
where the time goes in v1:
time: 165 us
  waiting for transfers between devices  59.1 us (36%)
  Pallas kernels  46.3 us (28%)
  starting transfers between devices  40.6 us (25%)
  local copies, waits for them, and re-layouts  10.4 us (6%)
  other arithmetic  6.91 us (4%)
    pallas_call x10, Pallas kernels, call(): pl.pallas_call(body, out_shape=shapes, in_specs=[near] * p + [far] * n, o...  46.3 us
    ppermute x8, waiting for transfers between devices, exchange(): came = lax.ppermute(x, ('dp', 'mp'), pairs)  37.4 us
    ppermute x7, waiting for transfers between devices, exchange(): return lax.ppermute(x, ('dp', 'mp'), pairs)  18.5 us
    ppermute x8, starting transfers between devices, exchange(): came = lax.ppermute(x, ('dp', 'mp'), pairs)  17.5 us
    ppermute x14, starting transfers between devices, swap(): return lax.ppermute(x, 'mp', [(0, 1), (1, 0)])  12 us
    ppermute x7, starting transfers between devices, exchange(): return lax.ppermute(x, ('dp', 'mp'), pairs)  11.1 us
    unnamed x40, local copies, waits for them, and re-layouts  5.94 us
  transfers between devices with their start and end apart: 29, of which 15 were waited for; matrix products, arithmetic and copies ran while one was open for 5% of the time, Pallas kernels for 22%

profile of v1, /device:TPU:0, one launch (start us, length us, event | category | flops | bytes accessed | tf_op | source)
XLA Modules:
  0.0 164.8 jit_solution(14370251117792430799)
XLA Ops:
  0.6 0.6 collective-permute-start
  1.3 0.4 collective-permute-start.2
  1.8 1.7 %copy.19.refs_1_ = s32[1024,1]{1,0:T(8,128)} copy(s32[1024,1]{0,1:T(1,128)} %bitcast.158) | data formatting | bytes 8192 | tf_op jit(solution)/shard_map/broadcast_in_dim | solution.py:517
  3.5 5.1 %shard_map.172 = (bf16[512,1024]{1,0:T(8,128)(2,1)}, bf16[512,512]{1,0:T(8,128)(2,1)}, f32[512,512]{1,0:T(8,128)}) custom-call(s32[1]{0:T(128)} %bitcast.2.refs_2_.refs_0_.refs_1_, s32[1024,1]{1,0:T(8,128)} %copy.19.refs_1_, s32[1,1024]{1,0:T(1,128)} %bitcast.161, s32[1,1024]{1,0:T(1,128)} %bitcast.162, bf16[1024,512]{1,0:T(8,128)(2,1)} %refs_4_.3), custom_call_target="tpu_custom_call" | custom-call | flops 1073741824 | bytes 3682304 | tf_op jit(solution)/shard_map/pallas_call | solution.py:133
  8.7 0.6 copy-done.15
  9.3 0.4 copy-done.12
  9.6 0.4 copy-done.3
  10.0 0.3 copy-done.4
  10.3 7.2 %shard_map.173 = (bf16[512,512]{1,0:T(8,128)(2,1)}, f32[512,512]{1,0:T(8,128)}, bf16[512,1024]{1,0:T(8,128)(2,1)}, f32[512,1024]{1,0:T(8,128)}, bf16[512,128]{1,...) custom-call(s32[1]{0:T(128)} %bitcast.2.refs_2_.refs_0_.refs_1_, ...), custom_call_target="tpu_custom_call" | custom-call | flops 3221225472 | bytes 14286848 | tf_op jit(solution)/shard_map/pallas_call | solution.py:133
  17.5 0.5 collective-permute-start.4
  18.1 0.4 collective-permute-start.20
  18.5 2.3 %shard_map.171 = bf16[16,24,128]{2,1,0:T(8,128)(2,1)} custom-call(s32[1]{0:T(128)} %bitcast.refs_0_, s32[16]{0:T(128)} %bitcast.159, s32[1]{0:T(128)} %bitcast.2.refs_2_.refs_0_.refs_1_, s32[16,32]{1,0:T(8,128)} %bitcast.157, bf16[16,32,128]{2,1,0:T(8,128)(2,1)} %bitcast.144), custom_call_target="tpu_custom_call" | custom-call | bytes 231424 | tf_op jit(solution)/shard_map/pallas_call | solution.py:133
  20.9 0.8 fusion.6
  21.8 0.8 copy-done.14
  22.6 0.3 copy-done.13
  22.9 4.0 %shard_map.174 = (bf16[512,512]{1,0:T(8,128)(2,1)}, bf16[512,512]{1,0:T(8,128)(2,1)}) custom-call(s32[1]{0:T(128)} %bitcast.7.refs_0_, bf16[512,1024]{1,0:T(8,128)(2,1)} %get-tuple-element.33.refs_1_, bf16[512,1024]{1,0:T(8,128)(2,1)} %copy-done.13, bf16[512,512]{1,0:T(8,128)(2,1)} %get-tuple-element.34.refs_3_.refs_0_, bf16[512,512]{1,0:T(8,128)(2,1)} %copy-done.14), custom_call_target="tpu_custom_call" | custom-call | flops 1073741824 | bytes 4194304 | tf_op jit(solution)/shard_map/pallas_call | solution.py:133
  26.9 1.1 pad_maximum_fusion.1
  28.0 2.6 %collective-permute-start.6 = (bf16[560,512]{1,0:T(8,128)(2,1)S(1)}, bf16[560,512]{1,0:T(8,128)(2,1)S(1)}, u32[]{:S(2)}, u32[]{:S(2)}) collective-permute-start(bf16[560,512]{1,0:T(8,128)(2,1)S(1)} %pad_maximum_fusion.1), channel_id=1, source_target_pairs={{0,2},{1,5},{2,0},{3,7},{4,6},{5,1},{6,4},{7,3},{8,10},{9,13},{10,... | collective-permute-start | bytes 1720328 | tf_op jit(solution)/shard_map/ppermute | solution.py:444
  30.6 6.3 %shard_map.177 = (bf16[512,1024]{1,0:T(8,128)(2,1)}, bf16[512,512]{1,0:T(8,128)(2,1)}, bf16[512,512]{1,0:T(8,128)(2,1)}) custom-call(bf16[512,512]{1,0:T(8,128)(2,1)} %get-tuple-element.34.refs_3_.refs_0_, bf16[512,512]{1,0:T(8,128)(2,1)} %get-tuple-element.35.refs_1_, bf16[1024,512]{1,0:T(8,128)(2,1)} %refs_2_.1, bf16[1024,512]{1,0:T(8,128)(2,1)} %copy-done.4, ...), custom_call_target="tpu_custom_call" | custom-call | flops 2147483648 | bytes 11534336 | tf_op jit(solution)/shard_map/pallas_call | solution.py:133
  36.9 0.2 collective-permute-start.18
  37.2 0.3 collective-permute-start.21
  37.7 0.6 collective-permute-done.6
  38.6 2.1 %collective-permute-start.7 = (bf16[304,512]{1,0:T(8,128)(2,1)S(1)}, bf16[304,512]{1,0:T(8,128)(2,1)S(1)}, u32[]{:S(2)}, u32[]{:S(2)}) collective-permute-start(bf16[304,512]{1,0:T(8,128)(2,1)S(1)} %pad_maximum_fusion.5), channel_id=1, source_target_pairs={{0,4},{1,3},{2,6},{3,1},{4,0},{5,7},{6,2},{7,5},{8,12},{9,11},{10,... | collective-permute-start | bytes 933896 | tf_op jit(solution)/shard_map/ppermute | solution.py:444
  40.7 0.7 collective-permute-done.17.refs_3_
  41.5 0.7 collective-permute-done.19.refs_7_
  42.2 6.2 %shard_map.178 = (bf16[256,2176]{1,0:T(8,128)(2,1)}, bf16[256,2176]{1,0:T(8,128)(2,1)}) custom-call(s32[1]{0:T(128)} %bitcast.51.refs_0_, s32[1]{0:T(128)} %bitcast.2.refs_2_.refs_0_.refs_1_, bf16[512,512]{1,0:T(8,128)(2,1)} %get-tuple-element.32.refs_3_.refs_2_, bf16[512,512]{1,0:T(8,128)(2,1)} %collective-permute-done.17.refs_3_, ...), custom_call_target="tpu_custom_call" | custom-call | flops 2147483648 | bytes 9830400 | tf_op jit(solution)/shard_map/pallas_call | solution.py:133
  48.5 1.3 collective-permute-start.22
  50.1 1.7 %collective-permute-start.8 = (bf16[176,512]{1,0:T(8,128)(2,1)S(1)}, bf16[176,512]{1,0:T(8,128)(2,1)S(1)}, u32[]{:S(2)}, u32[]{:S(2)}) collective-permute-start(bf16[176,512]{1,0:T(8,128)(2,1)S(1)} %pad_maximum_fusion.9), channel_id=1, source_target_pairs={{0,8},{1,9},{2,10},{3,11},{4,12},{5,13},{6,14},{7,15},{8,0},{9,1},... | collective-permute-start | bytes 540680 | tf_op jit(solution)/shard_map/ppermute | solution.py:444
  51.8 5.8 %collective-permute-done.8 = bf16[176,512]{1,0:T(8,128)(2,1)S(1)} collective-permute-done((bf16[176,512]{1,0:T(8,128)(2,1)S(1)}, bf16[176,512]{1,0:T(8,128)(2,1)S(1)}, u32[]{:S(2)}, u32[]{:S(2)}) %collective-permute-start.8) | collective-permute-done | bytes 180256 | tf_op jit(solution)/shard_map/ppermute | solution.py:444
  57.7 1.0 add_convert_fusion.6
  58.7 3.7 %collective-permute-start.9 = (bf16[176,512]{1,0:T(8,128)(2,1)S(1)}, bf16[176,512]{1,0:T(8,128)(2,1)S(1)}, u32[]{:S(2)}, u32[]{:S(2)}) collective-permute-start(bf16[176,512]{1,0:T(8,128)(2,1)S(1)} %pad_maximum_fusion.10), channel_id=1, source_target_pairs={{0,24},{1,25},{2,26},{3,27},{4,28},{5,29},{6,30},{7,31},{8,16},{9,... | collective-permute-start | bytes 540680 | tf_op jit(solution)/shard_map/ppermute | solution.py:444
  62.4 1.9 %collective-permute-done.22 = bf16[256,2176]{1,0:T(8,128)(2,1)S(1)} collective-permute-done((bf16[256,2176]{1,0:T(8,128)(2,1)}, bf16[256,2176]{1,0:T(8,128)(2,1)S(1)}, u32[]{:S(2)}, u32[]{:S(2)}) %collective-permute-start.22) | collective-permute-done | bytes 1114144 | tf_op jit(solution)/shard_map/ppermute | solution.py:439
  64.4 1.6 collective-permute-start.23
  66.0 2.0 %collective-permute-done.9 = bf16[176,512]{1,0:T(8,128)(2,1)S(1)} collective-permute-done((bf16[176,512]{1,0:T(8,128)(2,1)S(1)}, bf16[176,512]{1,0:T(8,128)(2,1)S(1)}, u32[]{:S(2)}, u32[]{:S(2)}) %collective-permute-start.9) | collective-permute-done | bytes 180256 | tf_op jit(solution)/shard_map/ppermute | solution.py:444
  68.1 9.0 %collective-permute-start.10 = (bf16[16,24,128]{2,1,0:T(8,128)(2,1)S(1)}, bf16[16,24,128]{2,1,0:T(8,128)(2,1)S(1)}, u32[]{:S(2)}, u32[]{:S(2)}) collective-permute-start(bf16[16,24,128]{2,1,0:T(8,128)(2,1)S(1)} %bitcast.116), channel_id=1, source_target_pairs={{0,1},{1,0},{2,3},{3,2},{4,5},{5,4},{6,7},{7,6},{8,9},{9,8},{10,11... | collective-permute-start | bytes 294920 | tf_op jit(solution)/shard_map/ppermute | solution.py:390
  77.2 0.7 add.115.refs_0_
  77.8 0.3 collective-permute-done.10.refs_3_
  78.1 0.6 copy-done.10
  78.7 6.7 %shard_map.175 = (bf16[16,16,128]{2,1,0:T(8,128)(2,1)}, f32[4096,128]{1,0:T(8,128)}) custom-call(s32[512]{0:T(512)} %add.115.refs_0_, s32[1]{0:T(128)} %bitcast.2.refs_2_.refs_0_.refs_1_, bf16[16,24,128]{2,1,0:T(8,128)(2,1)} %bitcast.117, bf16[16,24,128]{2,1,0:T(8,128)(2,1)} %copy-done.10, f32[4096,128]{1,0:T(8,128)} %refs_4_.5), custom_call_target="tpu_custom_call" | custom-call | bytes 4456448 | tf_op jit(solution)/shard_map/pallas_call | solution.py:133
  85.4 0.8 fusion.8
  86.2 3.4 %collective-permute-start.11 = (bf16[8,16,128]{2,1,0:T(8,128)(2,1)S(1)}, bf16[8,16,128]{2,1,0:T(8,128)(2,1)S(1)}, u32[]{:S(2)}, u32[]{:S(2)}) collective-permute-start(bf16[8,16,128]{2,1,0:T(8,128)(2,1)S(1)} %get-tuple-element.80), channel_id=1, source_target_pairs={{0,24},{1,25},{2,26},{3,27},{4,28},{5,29},{6,30},{7,31},{8,16},{9,... | collective-permute-start | bytes 98312 | tf_op jit(solution)/shard_map/ppermute | solution.py:444
  89.7 2.2 %collective-permute-done.11 = bf16[8,16,128]{2,1,0:T(8,128)(2,1)S(1)} collective-permute-done((bf16[8,16,128]{2,1,0:T(8,128)(2,1)S(1)}, bf16[8,16,128]{2,1,0:T(8,128)(2,1)S(1)}, u32[]{:S(2)}, u32[]{:S(2)}) %collective-permute-start.11) | collective-permute-done | bytes 32800 | tf_op jit(solution)/shard_map/ppermute | solution.py:444
  92.0 1.1 add_convert_fusion.3
  93.2 2.0 %collective-permute-start.12 = (bf16[160,512]{1,0:T(8,128)(2,1)S(1)}, bf16[160,512]{1,0:T(8,128)(2,1)S(1)}, u32[]{:S(2)}, u32[]{:S(2)}) collective-permute-start(bf16[160,512]{1,0:T(8,128)(2,1)S(1)} %pad_maximum_fusion.11), channel_id=1, source_target_pairs={{0,8},{1,9},{2,10},{3,11},{4,12},{5,13},{6,14},{7,15},{8,0},{9,1},... | collective-permute-start | bytes 491528 | tf_op jit(solution)/shard_map/ppermute | solution.py:444
  95.2 7.5 %collective-permute-done.12 = bf16[160,512]{1,0:T(8,128)(2,1)S(1)} collective-permute-done((bf16[160,512]{1,0:T(8,128)(2,1)S(1)}, bf16[160,512]{1,0:T(8,128)(2,1)S(1)}, u32[]{:S(2)}, u32[]{:S(2)}) %collective-permute-start.12) | collective-permute-done | bytes 163872 | tf_op jit(solution)/shard_map/ppermute | solution.py:444
  102.7 1.1 add_convert_fusion.2
  103.8 3.5 %collective-permute-start.25 = (bf16[64,2176]{1,0:T(8,128)(2,1)S(1)}, bf16[64,2176]{1,0:T(8,128)(2,1)S(1)}, u32[]{:S(2)}, u32[]{:S(2)}) collective-permute-start(bf16[64,2176]{1,0:T(8,128)(2,1)S(1)} %add_convert_fusion.2), channel_id=1, source_target_pairs={{0,24},{1,25},{2,26},{3,27},{4,28},{5,29},{6,30},{7,31},{8,16},{9,... | collective-permute-start | bytes 835592 | tf_op jit(solution)/shard_map/ppermute | solution.py:439
  107.4 4.9 %collective-permute-done.25 = bf16[64,2176]{1,0:T(8,128)(2,1)S(1)} collective-permute-done((bf16[64,2176]{1,0:T(8,128)(2,1)S(1)}, bf16[64,2176]{1,0:T(8,128)(2,1)S(1)}, u32[]{:S(2)}, u32[]{:S(2)}) %collective-permute-start.25) | collective-permute-done | bytes 278560 | tf_op jit(solution)/shard_map/ppermute | solution.py:439
  112.4 4.2 %collective-permute-start.26 = (bf16[64,2176]{1,0:T(8,128)(2,1)S(1)}, bf16[64,2176]{1,0:T(8,128)(2,1)S(1)}, u32[]{:S(2)}, u32[]{:S(2)}) collective-permute-start(bf16[64,2176]{1,0:T(8,128)(2,1)S(1)} %add_convert_fusion.1), channel_id=1, source_target_pairs={{0,8},{1,5},{2,10},{3,7},{4,12},{5,1},{6,14},{7,3},{8,0},{9,13},{1... | collective-permute-start | bytes 835592 | tf_op jit(solution)/shard_map/ppermute | solution.py:439
  116.7 4.4 %collective-permute-done.26 = bf16[64,2176]{1,0:T(8,128)(2,1)S(1)} collective-permute-done((bf16[64,2176]{1,0:T(8,128)(2,1)S(1)}, bf16[64,2176]{1,0:T(8,128)(2,1)S(1)}, u32[]{:S(2)}, u32[]{:S(2)}) %collective-permute-start.26) | collective-permute-done | bytes 278560 | tf_op jit(solution)/shard_map/ppermute | solution.py:439
  121.3 2.1 %collective-permute-done.13 = bf16[288,512]{1,0:T(8,128)(2,1)S(1)} collective-permute-done((bf16[288,512]{1,0:T(8,128)(2,1)S(1)}, bf16[288,512]{1,0:T(8,128)(2,1)S(1)}, u32[]{:S(2)}, u32[]{:S(2)}) %collective-permute-start.13) | collective-permute-done | bytes 294944 | tf_op jit(solution)/shard_map/ppermute | solution.py:444
  123.5 7.3 %collective-permute-done.27 = bf16[128,2176]{1,0:T(8,128)(2,1)S(1)} collective-permute-done((bf16[128,2176]{1,0:T(8,128)(2,1)S(1)}, bf16[128,2176]{1,0:T(8,128)(2,1)S(1)}, u32[]{:S(2)}, u32[]{:S(2)}) %collective-permute-start.27) | collective-permute-done | bytes 557088 | tf_op jit(solution)/shard_map/ppermute | solution.py:439
  131.1 0.2 collective-permute-start.28
  131.4 2.0 %collective-permute-start.14 = (bf16[544,512]{1,0:T(8,128)(2,1)S(1)}, bf16[544,512]{1,0:T(8,128)(2,1)S(1)}, u32[]{:S(2)}, u32[]{:S(2)}) collective-permute-start(bf16[544,512]{1,0:T(8,128)(2,1)S(1)} %pad_maximum_fusion.2), channel_id=1, source_target_pairs={{0,2},{1,5},{2,0},{3,7},{4,6},{5,1},{6,4},{7,3},{8,10},{9,13},{10,... | collective-permute-start | bytes 1671176 | tf_op jit(solution)/shard_map/ppermute | solution.py:444
  133.4 1.3 collective-permute-done.16
  134.8 0.7 pad_maximum_fusion.8
  135.5 17.1 %collective-permute-done.14.refs_2_ = bf16[544,512]{1,0:T(8,128)(2,1)S(1)} collective-permute-done((bf16[544,512]{1,0:T(8,128)(2,1)S(1)}, bf16[544,512]{1,0:T(8,128)(2,1)S(1)}, u32[]{:S(2)}, u32[]{:S(2)}) %collective-permute-start.14) | collective-permute-done | bytes 557088 | tf_op jit(solution)/shard_map/ppermute | solution.py:444
  152.6 0.8 copy-done.5
  153.6 0.8 pad_maximum_fusion.4.refs_1_
  154.4 2.8 %shard_map.180 = f32[1024,512]{1,0:T(8,128)} custom-call(s32[1]{0:T(128)} %bitcast.7.refs_0_, bf16[512,512]{1,0:T(8,128)(2,1)} %pad_maximum_fusion.4.refs_1_, bf16[544,512]{1,0:T(8,128)(2,1)} %copy-done.5), custom_call_target="tpu_custom_call" | custom-call | bytes 3178496 | tf_op jit(solution)/shard_map/pallas_call | solution.py:133
  157.2 0.6 copy-done.11
  157.9 2.3 %shard_map.176 = bf16[16,32,128]{2,1,0:T(8,128)(2,1)} custom-call(s32[1]{0:T(128)} %bitcast.refs_0_, s32[16]{0:T(128)} %bitcast.160, s32[1]{0:T(128)} %bitcast.2.refs_2_.refs_0_.refs_1_, bf16[16,16,128]{2,1,0:T(8,128)(2,1)} %bitcast.124, bf16[16,16,128]{2,1,0:T(8,128)(2,1)} %copy-done.11), custom_call_target="tpu_custom_call" | custom-call | bytes 262144 | tf_op jit(solution)/shard_map/pallas_call | solution.py:133
  160.2 1.0 copy-done.2
  161.2 3.5 %shard_map.179 = (f32[1024,512]{1,0:T(8,128)}, f32[512,1024]{1,0:T(8,128)}, f32[512,128]{1,0:T(8,128)}) custom-call(s32[1]{0:T(128)} %bitcast.51.refs_0_, bf16[256,2176]{1,0:T(8,128)(2,1)} %copy-done, bf16[256,2176]{1,0:T(8,128)(2,1)} %copy-done.2), custom_call_target="tpu_custom_call" | custom-call | bytes 6684672 | tf_op jit(solution)/shard_map/pallas_call | solution.py:133
  (118 shorter events, 2.6 us)
Async XLA Ops:
  0.6 8.0 %collective-permute-start = (bf16[1024,512]{1,0:T(8,128)(2,1)}, bf16[1024,512]{1,0:T(8,128)(2,1)S(1)}, u32[]{:S(2)}, u32[]{:S(2)}) collective-permute-start(bf16[1024,512]{1,0:T(8,128)(2,1)} %refs_4_.3), channel_id=1, source_target_pairs={{0,1},{1,0},{2,3},{3,2},{4,5},{5,4},{6,7},{7,6},{8,9},{9,8},{10,11... | collective-permute-start | bytes 3145736 | tf_op jit(solution)/shard_map/ppermute | solution.py:390
  1.2 7.4 %collective-permute-start.1 = (bf16[512,1024]{1,0:T(8,128)(2,1)}, bf16[512,1024]{1,0:T(8,128)(2,1)S(1)}, u32[]{:S(2)}, u32[]{:S(2)}) collective-permute-start(bf16[512,1024]{1,0:T(8,128)(2,1)} %refs_7_.1), channel_id=1, source_target_pairs={{0,1},{1,0},{2,3},{3,2},{4,5},{5,4},{6,7},{7,6},{8,9},{9,8},{10,11... | collective-permute-start | bytes 3145736 | tf_op jit(solution)/shard_map/ppermute | solution.py:390
  1.3 7.4 %collective-permute-start.2 = (bf16[1024,512]{1,0:T(8,128)(2,1)}, bf16[1024,512]{1,0:T(8,128)(2,1)S(1)}, u32[]{:S(2)}, u32[]{:S(2)}) collective-permute-start(bf16[1024,512]{1,0:T(8,128)(2,1)} %refs_2_.1), channel_id=1, source_target_pairs={{0,1},{1,0},{2,3},{3,2},{4,5},{5,4},{6,7},{7,6},{8,9},{9,8},{10,11... | collective-permute-start | bytes 3145736 | tf_op jit(solution)/shard_map/ppermute | solution.py:390
  1.7 6.9 %collective-permute-start.3 = (bf16[512,128]{1,0:T(8,128)(2,1)}, bf16[512,128]{1,0:T(8,128)(2,1)S(1)}, u32[]{:S(2)}, u32[]{:S(2)}) collective-permute-start(bf16[512,128]{1,0:T(8,128)(2,1)} %refs_8_.2), channel_id=1, source_target_pairs={{0,1},{1,0},{2,3},{3,2},{4,5},{5,4},{6,7},{7,6},{8,9},{9,8},{10,11... | collective-permute-start | bytes 393224 | tf_op jit(solution)/shard_map/ppermute | solution.py:390
  8.6 0.7 copy-start.15
  8.6 1.0 copy-start.12
  8.6 1.3 copy-start.3
  8.7 1.6 copy-start.4
  17.5 4.3 %collective-permute-start.4 = (bf16[512,1024]{1,0:T(8,128)(2,1)}, bf16[512,1024]{1,0:T(8,128)(2,1)S(1)}, u32[]{:S(2)}, u32[]{:S(2)}) collective-permute-start(bf16[512,1024]{1,0:T(8,128)(2,1)} %get-tuple-element.33.refs_1_), channel_id=1, source_target_pairs={{0,1},{1,0},{2,3},{3,2},{4,5},{5,4},{6,7},{7,6},{8,9},{9,8},{10,11... | collective-permute-start | bytes 3145736 | tf_op jit(solution)/shard_map/ppermute | solution.py:390
  18.0 3.8 %collective-permute-start.5 = (bf16[512,512]{1,0:T(8,128)(2,1)}, bf16[512,512]{1,0:T(8,128)(2,1)S(1)}, u32[]{:S(2)}, u32[]{:S(2)}) collective-permute-start(bf16[512,512]{1,0:T(8,128)(2,1)} %get-tuple-element.35.refs_1_), channel_id=1, source_target_pairs={{0,1},{1,0},{2,3},{3,2},{4,5},{5,4},{6,7},{7,6},{8,9},{9,8},{10,11... | collective-permute-start | bytes 1572872 | tf_op jit(solution)/shard_map/ppermute | solution.py:390
  18.1 20.5 %collective-permute-start.20 = (bf16[512,1024]{1,0:T(8,128)(2,1)}, bf16[512,1024]{1,0:T(8,128)(2,1)}, u32[]{:S(2)}, u32[]{:S(2)}) collective-permute-start(bf16[512,1024]{1,0:T(8,128)(2,1)} %get-tuple-element.31.refs_1_.refs_9_), channel_id=1, source_target_pairs={{0,1},{1,0},{2,3},{3,2},{4,5},{5,4},{6,7},{7,6},{8,9},{9,8},{10,11... | collective-permute-start | bytes 3145736 | tf_op jit(solution)/shard_map/ppermute | solution.py:390
  21.8 0.8 copy-start.14
  21.8 1.1 copy-start.13
  28.0 10.3 %collective-permute-start.6 = (bf16[560,512]{1,0:T(8,128)(2,1)S(1)}, bf16[560,512]{1,0:T(8,128)(2,1)S(1)}, u32[]{:S(2)}, u32[]{:S(2)}) collective-permute-start(bf16[560,512]{1,0:T(8,128)(2,1)S(1)} %pad_maximum_fusion.1), channel_id=1, source_target_pairs={{0,2},{1,5},{2,0},{3,7},{4,6},{5,1},{6,4},{7,3},{8,10},{9,13},{10,... | collective-permute-start | bytes 1720328 | tf_op jit(solution)/shard_map/ppermute | solution.py:444
  36.9 1.6 copy-start.6
  36.9 5.3 %collective-permute-start.18 = (bf16[512,1024]{1,0:T(8,128)(2,1)}, bf16[512,1024]{1,0:T(8,128)(2,1)}, u32[]{:S(2)}, u32[]{:S(2)}) collective-permute-start(bf16[512,1024]{1,0:T(8,128)(2,1)} %get-tuple-element.45.refs_4_), channel_id=1, source_target_pairs={{0,1},{1,0},{2,3},{3,2},{4,5},{5,4},{6,7},{7,6},{8,9},{9,8},{10,11... | collective-permute-start | bytes 3145736 | tf_op jit(solution)/shard_map/ppermute | solution.py:390
  37.2 3.6 %collective-permute-start.21 = (bf16[512,512]{1,0:T(8,128)(2,1)}, bf16[512,512]{1,0:T(8,128)(2,1)}, u32[]{:S(2)}, u32[]{:S(2)}) collective-permute-start(bf16[512,512]{1,0:T(8,128)(2,1)} %get-tuple-element.49), channel_id=1, source_target_pairs={{0,1},{1,0},{2,3},{3,2},{4,5},{5,4},{6,7},{7,6},{8,9},{9,8},{10,11... | collective-permute-start | bytes 1572872 | tf_op jit(solution)/shard_map/ppermute | solution.py:390
  37.5 4.0 %collective-permute-start.17 = (bf16[512,512]{1,0:T(8,128)(2,1)}, bf16[512,512]{1,0:T(8,128)(2,1)}, u32[]{:S(2)}, u32[]{:S(2)}) collective-permute-start(bf16[512,512]{1,0:T(8,128)(2,1)} %get-tuple-element.41), channel_id=1, source_target_pairs={{0,1},{1,0},{2,3},{3,2},{4,5},{5,4},{6,7},{7,6},{8,9},{9,8},{10,11... | collective-permute-start | bytes 1572872 | tf_op jit(solution)/shard_map/ppermute | solution.py:390
  38.3 3.9 %collective-permute-start.19 = (bf16[512,512]{1,0:T(8,128)(2,1)}, bf16[512,512]{1,0:T(8,128)(2,1)}, u32[]{:S(2)}, u32[]{:S(2)}) collective-permute-start(bf16[512,512]{1,0:T(8,128)(2,1)} %get-tuple-element.47), channel_id=1, source_target_pairs={{0,1},{1,0},{2,3},{3,2},{4,5},{5,4},{6,7},{7,6},{8,9},{9,8},{10,11... | collective-permute-start | bytes 1572872 | tf_op jit(solution)/shard_map/ppermute | solution.py:390
  38.6 11.2 %collective-permute-start.7 = (bf16[304,512]{1,0:T(8,128)(2,1)S(1)}, bf16[304,512]{1,0:T(8,128)(2,1)S(1)}, u32[]{:S(2)}, u32[]{:S(2)}) collective-permute-start(bf16[304,512]{1,0:T(8,128)(2,1)S(1)} %pad_maximum_fusion.5), channel_id=1, source_target_pairs={{0,4},{1,3},{2,6},{3,1},{4,0},{5,7},{6,2},{7,5},{8,12},{9,11},{10,... | collective-permute-start | bytes 933896 | tf_op jit(solution)/shard_map/ppermute | solution.py:444
  48.5 15.8 %collective-permute-start.22 = (bf16[256,2176]{1,0:T(8,128)(2,1)}, bf16[256,2176]{1,0:T(8,128)(2,1)S(1)}, u32[]{:S(2)}, u32[]{:S(2)}) collective-permute-start(bf16[256,2176]{1,0:T(8,128)(2,1)} %get-tuple-element.51), channel_id=1, source_target_pairs={{0,2},{1,9},{2,0},{3,11},{4,6},{5,13},{6,4},{7,15},{8,10},{9,1},{1... | collective-permute-start | bytes 3342344 | tf_op jit(solution)/shard_map/ppermute | solution.py:439
  50.1 14.2 %copy-start.1 = (bf16[256,2176]{1,0:T(8,128)(2,1)S(1)}, bf16[256,2176]{1,0:T(8,128)(2,1)}, u32[]{:S(2)}) copy-start(bf16[256,2176]{1,0:T(8,128)(2,1)} %get-tuple-element.50) | copy-start | bytes 3342340
  50.1 7.5 %collective-permute-start.8 = (bf16[176,512]{1,0:T(8,128)(2,1)S(1)}, bf16[176,512]{1,0:T(8,128)(2,1)S(1)}, u32[]{:S(2)}, u32[]{:S(2)}) collective-permute-start(bf16[176,512]{1,0:T(8,128)(2,1)S(1)} %pad_maximum_fusion.9), channel_id=1, source_target_pairs={{0,8},{1,9},{2,10},{3,11},{4,12},{5,13},{6,14},{7,15},{8,0},{9,1},... | collective-permute-start | bytes 540680 | tf_op jit(solution)/shard_map/ppermute | solution.py:444
  58.7 9.3 %collective-permute-start.9 = (bf16[176,512]{1,0:T(8,128)(2,1)S(1)}, bf16[176,512]{1,0:T(8,128)(2,1)S(1)}, u32[]{:S(2)}, u32[]{:S(2)}) collective-permute-start(bf16[176,512]{1,0:T(8,128)(2,1)S(1)} %pad_maximum_fusion.10), channel_id=1, source_target_pairs={{0,24},{1,25},{2,26},{3,27},{4,28},{5,29},{6,30},{7,31},{8,16},{9,... | collective-permute-start | bytes 540680 | tf_op jit(solution)/shard_map/ppermute | solution.py:444
  64.4 27.6 %collective-permute-start.23 = (bf16[128,2176]{1,0:T(8,128)(2,1)S(1)}, bf16[128,2176]{1,0:T(8,128)(2,1)}, u32[]{:S(2)}, u32[]{:S(2)}) collective-permute-start(bf16[128,2176]{1,0:T(8,128)(2,1)S(1)} %add_convert_fusion), channel_id=1, source_target_pairs={{0,4},{1,3},{2,6},{3,1},{4,0},{5,7},{6,2},{7,5},{8,12},{9,11},{10,... | collective-permute-start | bytes 1671176 | tf_op jit(solution)/shard_map/ppermute | solution.py:439
  68.1 10.0 %copy-start.7 = (bf16[1,2,8,24,128]{4,3,2,1,0:T(8,128)(2,1)}, bf16[1,2,8,24,128]{4,3,2,1,0:T(8,128)(2,1)S(1)}, u32[]{:S(2)}) copy-start(bf16[1,2,8,24,128]{4,3,2,1,0:T(8,128)(2,1)S(1)} %pad_maximum_fusion.14) | copy-start | bytes 294916
  68.1 10.0 %collective-permute-start.10 = (bf16[16,24,128]{2,1,0:T(8,128)(2,1)S(1)}, bf16[16,24,128]{2,1,0:T(8,128)(2,1)S(1)}, u32[]{:S(2)}, u32[]{:S(2)}) collective-permute-start(bf16[16,24,128]{2,1,0:T(8,128)(2,1)S(1)} %bitcast.116), channel_id=1, source_target_pairs={{0,1},{1,0},{2,3},{3,2},{4,5},{5,4},{6,7},{7,6},{8,9},{9,8},{10,11... | collective-permute-start | bytes 294920 | tf_op jit(solution)/shard_map/ppermute | solution.py:390
  78.1 0.6 copy-start.10
  86.2 5.7 %collective-permute-start.11 = (bf16[8,16,128]{2,1,0:T(8,128)(2,1)S(1)}, bf16[8,16,128]{2,1,0:T(8,128)(2,1)S(1)}, u32[]{:S(2)}, u32[]{:S(2)}) collective-permute-start(bf16[8,16,128]{2,1,0:T(8,128)(2,1)S(1)} %get-tuple-element.80), channel_id=1, source_target_pairs={{0,24},{1,25},{2,26},{3,27},{4,28},{5,29},{6,30},{7,31},{8,16},{9,... | collective-permute-start | bytes 98312 | tf_op jit(solution)/shard_map/ppermute | solution.py:444
  93.0 9.7 %collective-permute-start.24 = (bf16[64,2176]{1,0:T(8,128)(2,1)S(1)}, bf16[64,2176]{1,0:T(8,128)(2,1)S(1)}, u32[]{:S(2)}, u32[]{:S(2)}) collective-permute-start(bf16[64,2176]{1,0:T(8,128)(2,1)S(1)} %add_convert_fusion.3), channel_id=1, source_target_pairs={{0,8},{1,5},{2,10},{3,7},{4,12},{5,1},{6,14},{7,3},{8,0},{9,13},{1... | collective-permute-start | bytes 835592 | tf_op jit(solution)/shard_map/ppermute | solution.py:439
  93.2 9.4 %collective-permute-start.12 = (bf16[160,512]{1,0:T(8,128)(2,1)S(1)}, bf16[160,512]{1,0:T(8,128)(2,1)S(1)}, u32[]{:S(2)}, u32[]{:S(2)}) collective-permute-start(bf16[160,512]{1,0:T(8,128)(2,1)S(1)} %pad_maximum_fusion.11), channel_id=1, source_target_pairs={{0,8},{1,9},{2,10},{3,11},{4,12},{5,13},{6,14},{7,15},{8,0},{9,1},... | collective-permute-start | bytes 491528 | tf_op jit(solution)/shard_map/ppermute | solution.py:444
  103.8 8.5 %collective-permute-start.25 = (bf16[64,2176]{1,0:T(8,128)(2,1)S(1)}, bf16[64,2176]{1,0:T(8,128)(2,1)S(1)}, u32[]{:S(2)}, u32[]{:S(2)}) collective-permute-start(bf16[64,2176]{1,0:T(8,128)(2,1)S(1)} %add_convert_fusion.2), channel_id=1, source_target_pairs={{0,24},{1,25},{2,26},{3,27},{4,28},{5,29},{6,30},{7,31},{8,16},{9,... | collective-permute-start | bytes 835592 | tf_op jit(solution)/shard_map/ppermute | solution.py:439
  112.4 8.7 %collective-permute-start.26 = (bf16[64,2176]{1,0:T(8,128)(2,1)S(1)}, bf16[64,2176]{1,0:T(8,128)(2,1)S(1)}, u32[]{:S(2)}, u32[]{:S(2)}) collective-permute-start(bf16[64,2176]{1,0:T(8,128)(2,1)S(1)} %add_convert_fusion.1), channel_id=1, source_target_pairs={{0,8},{1,5},{2,10},{3,7},{4,12},{5,1},{6,14},{7,3},{8,0},{9,13},{1... | collective-permute-start | bytes 835592 | tf_op jit(solution)/shard_map/ppermute | solution.py:439
  116.6 6.8 %collective-permute-start.13 = (bf16[288,512]{1,0:T(8,128)(2,1)S(1)}, bf16[288,512]{1,0:T(8,128)(2,1)S(1)}, u32[]{:S(2)}, u32[]{:S(2)}) collective-permute-start(bf16[288,512]{1,0:T(8,128)(2,1)S(1)} %pad_maximum_fusion.6), channel_id=1, source_target_pairs={{0,4},{1,3},{2,6},{3,1},{4,0},{5,7},{6,2},{7,5},{8,12},{9,11},{10,... | collective-permute-start | bytes 884744 | tf_op jit(solution)/shard_map/ppermute | solution.py:444
  121.2 9.6 %collective-permute-start.27 = (bf16[128,2176]{1,0:T(8,128)(2,1)S(1)}, bf16[128,2176]{1,0:T(8,128)(2,1)S(1)}, u32[]{:S(2)}, u32[]{:S(2)}) collective-permute-start(bf16[128,2176]{1,0:T(8,128)(2,1)S(1)} %pad_maximum_fusion.3), channel_id=1, source_target_pairs={{0,4},{1,3},{2,6},{3,1},{4,0},{5,7},{6,2},{7,5},{8,12},{9,11},{10,... | collective-permute-start | bytes 1671176 | tf_op jit(solution)/shard_map/ppermute | solution.py:439
  131.1 3.7 %copy-start = (bf16[256,2176]{1,0:T(8,128)(2,1)}, bf16[256,2176]{1,0:T(8,128)(2,1)S(1)}, u32[]{:S(2)}) copy-start(bf16[256,2176]{1,0:T(8,128)(2,1)S(1)} %pad_maximum_fusion.refs_1_) | copy-start | bytes 3342340
  131.1 2.3 %copy-start.9 = (bf16[512,128]{1,0:T(8,128)(2,1)S(1)}, bf16[512,128]{1,0:T(8,128)(2,1)}, u32[]{:S(2)}) copy-start(bf16[512,128]{1,0:T(8,128)(2,1)} %get-tuple-element.40) | copy-start | bytes 393220
  131.1 29.1 %collective-permute-start.28 = (bf16[256,2176]{1,0:T(8,128)(2,1)S(1)}, bf16[256,2176]{1,0:T(8,128)(2,1)S(1)}, u32[]{:S(2)}, u32[]{:S(2)}) collective-permute-start(bf16[256,2176]{1,0:T(8,128)(2,1)S(1)} %pad_maximum_fusion.refs_1_), channel_id=1, source_target_pairs={{0,2},{1,9},{2,0},{3,11},{4,6},{5,13},{6,4},{7,15},{8,10},{9,1},{1... | collective-permute-start | bytes 3342344 | tf_op jit(solution)/shard_map/ppermute | solution.py:439
  131.4 21.2 %collective-permute-start.14 = (bf16[544,512]{1,0:T(8,128)(2,1)S(1)}, bf16[544,512]{1,0:T(8,128)(2,1)S(1)}, u32[]{:S(2)}, u32[]{:S(2)}) collective-permute-start(bf16[544,512]{1,0:T(8,128)(2,1)S(1)} %pad_maximum_fusion.2), channel_id=1, source_target_pairs={{0,2},{1,5},{2,0},{3,7},{4,6},{5,1},{6,4},{7,3},{8,10},{9,13},{10,... | collective-permute-start | bytes 1671176 | tf_op jit(solution)/shard_map/ppermute | solution.py:444
  133.4 1.3 collective-permute-start.16
  152.6 0.8 copy-start.5
  153.5 3.7 %copy-start.8 = (bf16[8,2,1,16,128]{4,3,1,0,2:T(8,128)(2,1)}, bf16[8,2,1,16,128]{4,3,1,0,2:T(8,128)(2,1)S(1)}, u32[]{:S(2)}) copy-start(bf16[8,2,1,16,128]{4,3,1,0,2:T(8,128)(2,1)S(1)} %copy.41) | copy-start | bytes 196612
  153.5 3.7 %collective-permute-start.15 = (bf16[16,16,128]{2,1,0:T(8,128)(2,1)S(1)}, bf16[16,16,128]{2,1,0:T(8,128)(2,1)S(1)}, u32[]{:S(2)}, u32[]{:S(2)}) collective-permute-start(bf16[16,16,128]{2,1,0:T(8,128)(2,1)S(1)} %bitcast.123), channel_id=1, source_target_pairs={{0,1},{1,0},{2,3},{3,2},{4,5},{5,4},{6,7},{7,6},{8,9},{9,8},{10,11... | collective-permute-start | bytes 196616 | tf_op jit(solution)/shard_map/ppermute | solution.py:390
  157.2 0.6 copy-start.11
  160.2 1.0 copy-start.2
